TPU v7x, 128 devices: a whole 4x4x4 slice. The times are simulated.
128 devices in a mesh: dp: 2 (over core), seq: 4 (over x), tensor: 16 (over y, z).
Axes of the slice: x: 4, y: 4, z: 4, core: 2. Of those that a mesh axis runs over, the one named last changes fastest.
Arguments:
- tokens: bfloat16 [16384, 4096], P(('dp', 'seq', 'tensor')), may hold values from -6 to 6
- cotangent: bfloat16 [16384, 14336], P(('dp', 'seq', 'tensor')), may hold values from -0.046875 to 0.046875
- master: bfloat16 [8, 336, 128, 128], P(None, 'tensor'), as said below
- block_ids: int32 [8, 336], P(None, 'tensor'), may hold values from 0 to 223, as said below
- live_count: int32 [8, 16], P(None, 'tensor'), may hold values from 1 to 21, as said below
Outputs:
- outputs: bfloat16 [16384, 14336], P(('dp', 'seq', 'tensor'))
- w_grad: float32 [8, 336, 128, 128], P(('dp', 'seq'), 'tensor')
Inputs may be any that keep to these rules, and one draw needn't show every extreme that they name: Within each group t the 168 entries block_ids[:, t * 21 : (t + 1) * 21] are distinct. `live_count`: in every group one owner uses all 21 slots. `master`: in every block one entry has the largest magnitude, and no entry of a block, divided by that magnitude over 7, lies within 0.1 of a half-integer.
All inputs are finite; a program needn't handle non-finite values. Where the computation divides by a largest or mean magnitude, that divisor is 1e-20 or more.
Results may differ from a plain program's by a relative error of at most 0.005.
Values may be sent and summed in bfloat16 or wider, within the bound.
A program may use at most 192 MiB of HBM per device.

v0:
```python
import jax
import jax.numpy as jnp
from jax import lax
from jax.sharding import PartitionSpec as P

BS = 128


def fake_quant(master, live_mask):
    master_wide = master.astype(jnp.float32)
    block_peak = jnp.max(jnp.abs(master_wide), axis=(-2, -1), keepdims=True) + 1e-06
    levels = jnp.floor(master_wide * (7.0 / block_peak) + 0.5)
    return (levels * (block_peak / 7.0) * live_mask[..., None, None]).astype(jnp.bfloat16)


def assemble(quantized, slot_ids, row_blocks, col_blocks):
    total_slots = quantized.shape[0]
    block_numbers = jnp.arange(row_blocks * col_blocks, dtype=jnp.int32)
    slot_numbers = jnp.arange(1, total_slots + 1, dtype=jnp.int32)
    matches = (slot_ids[:, None] == block_numbers[None, :]).astype(jnp.int32)
    slot_of_block = jnp.sum(matches * slot_numbers[:, None], axis=0)
    padded = jnp.concatenate([jnp.zeros((1, BS, BS), jnp.bfloat16), quantized], axis=0)
    placed = jnp.take(padded, slot_of_block, axis=0).reshape(row_blocks, col_blocks, BS, BS)
    return placed.transpose(0, 2, 1, 3).reshape(row_blocks * BS, col_blocks * BS)


def dense_gradient(token_rows, grad_rows):
    return lax.dot_general(
        token_rows, grad_rows, (((0,), (0,)), ((), ())), preferred_element_type=jnp.float32
    )


def pick_blocks(full_grad, slot_ids, row_blocks, col_blocks):
    grid_blocks = full_grad.reshape(row_blocks, BS, col_blocks, BS).transpose(0, 2, 1, 3)
    grid_blocks = grid_blocks.reshape(row_blocks * col_blocks, BS, BS)
    return jnp.take(grid_blocks, slot_ids, axis=0)


def shards(tokens, cotangent, master, block_ids, live_count):
    owners, slots = block_ids.shape
    groups = lax.axis_size("tensor")
    live_mask = (jnp.arange(slots, dtype=jnp.int32)[None, :] < live_count).astype(jnp.float32)
    quantized = fake_quant(master, live_mask).reshape(owners * slots, BS, BS)
    slot_ids = block_ids.reshape(owners * slots)
    row_blocks = tokens.shape[1] // BS
    col_blocks = cotangent.shape[1] // (BS * groups)
    dense_weight = assemble(quantized, slot_ids, row_blocks, col_blocks)
    grads_local = lax.all_to_all(cotangent, "tensor", split_axis=1, concat_axis=0, tiled=True)
    gathered = lax.all_gather(tokens, "tensor", axis=0, tiled=True)
    results = jnp.dot(gathered, dense_weight, preferred_element_type=jnp.float32)
    full_grad = dense_gradient(gathered, grads_local)
    outputs = lax.all_to_all(
        results.astype(jnp.bfloat16), "tensor", split_axis=0, concat_axis=1, tiled=True
    )
    partial_value = pick_blocks(full_grad, slot_ids, row_blocks, col_blocks)
    partial_value = (partial_value * live_mask.reshape(owners * slots)[:, None, None]).reshape(
        owners, slots, BS, BS
    )
    w_grad = lax.psum_scatter(partial_value, ("dp", "seq"), scatter_dimension=0, tiled=True)
    return (outputs, w_grad)


def solution(mesh):
    return jax.shard_map(
        shards,
        mesh=mesh,
        in_specs=(
            P(("dp", "seq", "tensor"), None),
            P(("dp", "seq", "tensor"), None),
            P(None, "tensor", None, None),
            P(None, "tensor"),
            P(None, "tensor"),
        ),
        out_specs=(P(("dp", "seq", "tensor"), None), P(("dp", "seq"), "tensor", None, None)),
        check_vma=False,
    )
```

profile of v0, /device:TPU:9, one launch (start us, length us, event | category | flops | bytes accessed | tf_op | source)
XLA Modules:
  0.0 368.8 jit_solution(11243594162319001183)
XLA Ops:
  7.2 0.0 all-gather.2.cloned.1.call-start
  7.2 0.7 all-gather.2.cloned.1.call-update
  7.9 6.1 %copy.33 = bf16[128,14336]{0,1:T(8,128)(2,1)} copy(bf16[128,14336]{1,0:T(8,128)(2,1)} %param.6) | data formatting | bytes 7340032 | tf_op args[1]
  13.9 0.0 copy-start
  14.0 6.1 %copy.34 = bf16[128,16,896]{2,0,1:T(8,128)(2,1)} copy(bf16[128,16,896]{0,2,1:T(8,128)(2,1)} %bitcast.55) | data formatting | bytes 7340032 | tf_op jit(solution)/shard_map/all_to_all | solution.py:48
  20.1 7.8 %all-to-all-start.1 = ((bf16[128,16,896]{2,0,1:T(8,128)(2,1)}), bf16[128,16,896]{2,0,1:T(8,128)(2,1)}, u32[]{:S(2)}, u32[]{:S(2)}) async-start(bf16[128,16,896]{2,0,1:T(8,128)(2,1)} %copy.34), calls=%async_computation.1 | async-start | bytes 7340032 | tf_op jit(solution)/shard_map/all_to_all | solution.py:48
  27.9 0.0 reduce-scatter.2.cloned.1.call-start
  28.0 0.0 copy-done
  28.0 0.1 reshape.139
  28.1 0.0 copy-done.1
  28.1 0.1 fusion.11
  28.2 3.9 %fusion = f32[8,21]{1,0:T(8,128)S(1)} fusion(bf16[8,21,128,128]{3,2,1,0:T(8,128)(2,1)} %param.7), kind=kLoop, calls=%fused_computation.4 | loop fusion | flops 8257368 | bytes 5505696 | tf_op jit(solution)/shard_map/reduce_max | solution.py:11
  32.1 54.9 %all-to-all-done.1 = bf16[128,16,896]{2,0,1:T(8,128)(2,1)} async-done(((bf16[128,16,896]{2,0,1:T(8,128)(2,1)}), bf16[128,16,896]{2,0,1:T(8,128)(2,1)}, u32[]{:S(2)}, u32[]{:S(2)}) %all-to-all-start.1) | async-done | bytes 3670048 | tf_op jit(solution)/shard_map/all_to_all | solution.py:48
  87.0 6.1 %copy.35 = bf16[2048,896]{0,1:T(8,128)(2,1)} copy(bf16[2048,896]{1,0:T(8,128)(2,1)} %bitcast.15) | data formatting | bytes 7340032 | tf_op jit(solution)/shard_map/all_to_all | solution.py:48
  93.1 71.8 %all-gather.2.cloned.1.call-done = bf16[2048,4096]{1,0:T(8,128)(2,1)} async-done(((bf16[128,4096]{1,0:T(8,128)(2,1)}), bf16[2048,4096]{1,0:T(8,128)(2,1)}) %all-gather.2.cloned.1.call-update) | async-done | bytes 16777232 | tf_op jit(solution)/shard_map/all_gather | solution.py:49
  164.9 22.5 %copy.32 = bf16[4096,2048]{1,0:T(8,128)(2,1)} copy(bf16[4096,2048]{0,1:T(8,128)(2,1)} %bitcast.51) | data formatting | bytes 33554432 | tf_op jit(solution)/shard_map/dot_general | solution.py:28
  187.4 23.3 %fusion.12 = f32[32,128,7,128]{3,1,2,0:T(8,128)} fusion(bf16[32,128,2048,1]{2,1,3,0:T(8,128)(2,1)} %bitcast.52, bf16[7,128,2048,1]{2,1,0,3:T(8,128)(2,1)} %bitcast.58), kind=kOutput, calls=%fused_computation.32 | convolution fusion | flops 15032385536 | bytes 35127296 | tf_op jit(solution)/shard_map/dot_general | solution.py:28
  210.7 15.5 %gather_fusion.1 = f32[168,128,128]{2,1,0:T(8,128)} fusion(f32[224,128,128]{2,1,0:T(8,128)} %bitcast.56, s32[1024]{0:T(1024)S(1)} %pad_clamp_fusion), kind=kCustom, calls=%fused_computation.1 | custom fusion | bytes 22020768 | tf_op jit(solution)/shard_map/jit(_take)/gather | solution.py:36
  226.2 14.1 %select_multiply_fusion = (f32[8,21,128,128]{3,2,1,0:T(8,128)}, bf16[8,21,128,128]{3,2,1,0:T(8,128)(2,1)}) fusion(f32[8,21,128,128]{3,2,1,0:T(8,128)} %bitcast.48, f32[8,21]{1,0:T(8,128)S(1)} %get-tuple-element.12, pred[8,21]{1,0:T(8,128)(4,1)S(1)} %get-tuple-element.13, f32[8,21]{1,0:T(8,128)S(1)} %get-tuple-element.11, f32[8,21]{1,0:T(8,128)S(1)} %get-tuple-element.10, ...), kind=kLoop, calls=%fused_computation.10 | loop fusion | flops 24772608 | bytes 33032328 | tf_op jit(solution)/shard_map/mul | solution.py:56
  240.4 0.0 reduce-scatter.2.cloned.1.call-update
  240.4 0.1 eq.15
  240.5 0.1 select_reduce_fusion
  240.6 0.1 reduce_sum.14
  240.7 7.2 %concatenate.3 = bf16[169,128,128]{2,1,0:T(8,128)(2,1)} pad(bf16[168,128,128]{2,1,0:T(8,128)(2,1)} %bitcast.50, bf16[]{:T(256)} %constant.42.clone.1), padding=1_0x0_0x0_0 | pad | bytes 11042818 | tf_op jit(solution)/shard_map/concatenate | solution.py:22
  247.9 11.1 %gather_fusion = bf16[224,128,128]{2,1,0:T(8,128)(2,1)} fusion(bf16[169,128,128]{2,1,0:T(8,128)(2,1)} %concatenate.3, s32[1024]{0:T(1024)S(1)} %pad_clamp_fusion.1), kind=kCustom, calls=%fused_computation | custom fusion | bytes 14680960 | tf_op jit(solution)/shard_map/jit(_take)/gather | solution.py:23
  259.0 6.8 %select_bitcast_fusion = bf16[32,128,7,128]{3,1,2,0:T(8,128)(2,1)} fusion(bf16[32,7,128,128]{3,2,1,0:T(8,128)(2,1)} %bitcast.49, pred[32,7]{1,0:T(8,128)(4,1)S(1)} %compare_and_fusion), kind=kLoop, calls=%fused_computation.14 | loop fusion | flops 3670016 | bytes 14680288 | tf_op jit(solution)/shard_map/transpose | solution.py:24
  265.8 12.3 %copy.30 = bf16[32,128,7,128]{1,0,3,2:T(8,128)(2,1)} copy(bf16[32,128,7,128]{3,1,2,0:T(8,128)(2,1)} %select_bitcast_fusion) | data formatting | bytes 14680064 | tf_op jit(solution)/shard_map/transpose | solution.py:24
  278.0 21.0 %convert_bitcast_fusion = bf16[112,16,8,128]{3,2,1,0:T(8,128)(2,1)S(1)} fusion(bf16[2048,4096]{1,0:T(8,128)(2,1)} %all-gather.2.cloned.1.call-done, bf16[112,8,32,128]{3,2,1,0:T(8,128)(2,1)} %bitcast.57), kind=kOutput, calls=%fused_computation.16 | convolution fusion | flops 15034220544 | bytes 27787264 | tf_op jit(solution)/shard_map/dot_general | solution.py:50
  299.0 0.9 copy.47
  300.0 53.3 %all_to_all.38 = bf16[16,128,896]{1,2,0:T(8,128)(2,1)} all-to-all(bf16[16,128,896]{1,2,0:T(8,128)(2,1)S(1)} %bitcast.53), channel_id=1, replica_groups=mesh['dp'=2,'seq'=4,'tensor'=16] {'tensor'}, dimensions={0} | all-to-all | bytes 7340032 | tf_op jit(solution)/shard_map/all_to_all | solution.py:52
  353.3 6.1 %copy.36 = bf16[128,14336]{1,0:T(8,128)(2,1)} copy(bf16[128,14336]{0,1:T(8,128)(2,1)} %bitcast.54) | data formatting | bytes 7340032
  359.3 2.6 reduce-scatter.2.cloned.1.call-done
  (8 shorter events, 0.0 us)
Async XLA Ops:
  7.2 157.7 %all-gather.2.cloned.1.call-start = ((), (), s32[]{:S(2)}) async-start(), calls=%async_computation.3 | async-start | bytes 17825792 | tf_op jit(solution)/shard_map/all_gather | solution.py:49
  13.9 14.0 %copy-start = (s32[8,21]{1,0:T(8,128)S(1)}, s32[8,21]{1,0:T(8,128)}, u32[]{:S(2)}) copy-start(s32[8,21]{1,0:T(8,128)} %param.8) | copy-start | bytes 2020
  13.9 14.1 %copy-start.1 = (s32[8,1]{0,1:T(1,128)S(1)}, s32[8,1]{0,1:T(1,128)}, u32[]{:S(2)}) copy-start(s32[8,1]{0,1:T(1,128)} %param.9) | copy-start | bytes 100
  20.1 67.0 %all-to-all-start.1 = ((bf16[128,16,896]{2,0,1:T(8,128)(2,1)}), bf16[128,16,896]{2,0,1:T(8,128)(2,1)}, u32[]{:S(2)}, u32[]{:S(2)}) async-start(bf16[128,16,896]{2,0,1:T(8,128)(2,1)} %copy.34), calls=%async_computation.1 | async-start | bytes 7340032 | tf_op jit(solution)/shard_map/all_to_all | solution.py:48
  27.9 334.0 %reduce-scatter.2.cloned.1.call-start = ((), (), s32[]{:S(2)}) async-start(), calls=%async_computation.4 | async-start | bytes 12386304 | tf_op jit(solution)/shard_map/reduce_scatter | solution.py:59
Sparse Core Ops, SparseCore 0:
  10.1 154.7 all-gather.1
  240.5 121.3 reduce-scatter.1
where the time goes:
time: 371 us; the launch traced here: 369 us
  waiting for transfers between devices  130 us (35%)
  local copies, waits for them, and re-layouts  94.1 us (25%)
  blocking collectives  53.3 us (14%)
  matrix products  44.3 us (12%)
  other arithmetic  25.1 us (7%)
  between operations  14.1 us (4%)
  starting transfers between devices  7.92 us (2%)
    all_gather x1, waiting for transfers between devices, shards(): gathered = lax.all_gather(tokens, 'tensor', axis=0, tiled=True)  71.8 us
    all_to_all x1, waiting for transfers between devices, shards(): lax.all_to_all(cotangent, 'tensor', split_axis=1, concat_axis=0, tiled=True)  54.9 us
    all_to_all x1, blocking collectives, shards(): lax.all_to_all(results.astype(jnp.bfloat16), 'tensor', split_axis=0, conc...  53.3 us
    dot_general x1, matrix products, dense_gradient(): lax.dot_general(token_rows, grad_rows, (((0,), (0,)), ((), ())), preferre...  23.3 us
    dot_general x1, local copies, waits for them, and re-layouts, dense_gradient(): lax.dot_general(token_rows, grad_rows, (((0,), (0,)), ((), ())), preferre...  22.5 us
    dot_general x1, matrix products, shards(): jnp.dot(gathered, dense_weight, preferred_element_type=jnp.float32)  21 us
    gather x1, local copies, waits for them, and re-layouts, pick_blocks(): return jnp.take(grid_blocks, slot_ids, axis=0)  15.5 us
    mul x1, other arithmetic, shards(): partial_value * live_mask.reshape(owners * slots)[:, None, None]  14.1 us
  transfers between devices with their start and end apart: 3, of which 3 were waited for; matrix products, arithmetic and copies ran while one was open for 24% of the time, Pallas kernels for 0%

commit v1 on v0

v1 whole, which is shorter than its diff:
```python
import functools

import jax
import jax.numpy as jnp
from jax import lax
from jax.experimental import pallas as pl
from jax.experimental.pallas import tpu as pltpu
from jax.sharding import PartitionSpec as P

BS = 128
ROWS = 32
COLS = 7
OWN = 8
SLOTS = 21
NSLOT = OWN * SLOTS
QTR = NSLOT // 4
HALF = QTR // 2
LO, HI = 11, 10
WID = COLS * BS
TOK = 128
MESH = pl.DeviceIdType.MESH
F32 = jnp.float32
BF16 = jnp.bfloat16


class Names:
    def __init__(self):
        self.n = 0
        self.at = {}

    def get(self, key, width=1):
        if key not in self.at:
            self.at[key] = self.n
            self.n += width
        return self.at[key]


def fake_quant(master, live_mask):
    master_wide = master.astype(jnp.float32)
    block_peak = jnp.max(jnp.abs(master_wide), axis=(-2, -1), keepdims=True) + 1e-06
    levels = jnp.floor(master_wide * (7.0 / block_peak) + 0.5)
    return (levels * (block_peak / 7.0) * live_mask[..., None, None]).astype(jnp.bfloat16)


def make_kernel(names_s, names_r, names_l):
    def kernel(
        tok_hbm, cot_hbm, q_hbm, tab_hbm,
        out_hbm, wg_hbm, wc_hbm,
        tok_v, cb, crel, gw, wst, ob, orel, gs, ra1, ra2, ry1, ry2, rz1, rz2, rb1, rb2, fin,
        tabv, tabs, ssem, rsem, lsem,
    ):
        k = lax.axis_index("dp")
        x = lax.axis_index("seq")
        t_me = lax.axis_index("tensor")
        y, z = t_me // 4, t_me % 4
        xp, xm, xo = (x + 1) % 4, (x + 3) % 4, (x + 2) % 4
        yp, ym, yo = (y + 1) % 4, (y + 3) % 4, (y + 2) % 4
        zp, zm, zo = (z + 1) % 4, (z + 3) % 4, (z + 2) % 4
        kk = 1 - k

        def dev(k_=None, x_=None, y_=None, z_=None):
            kd = k if k_ is None else k_
            xd = x if x_ is None else x_
            yd = y if y_ is None else y_
            zd = z if z_ is None else z_
            return (kd, xd, yd * 4 + zd)

        partner = dev(k_=kk)
        devs = {
            "x+": dev(x_=xp), "x-": dev(x_=xm), "y+": dev(y_=yp), "y-": dev(y_=ym), "y2": dev(y_=yo),
            "z+": dev(z_=zp), "z-": dev(z_=zm), "p": partner,
            "z+0": dev(k_=0, z_=zp), "z+1": dev(k_=1, z_=zp), "z-0": dev(k_=0, z_=zm), "z-1": dev(k_=1, z_=zm),
        }

        def remote(key, src, dst, to, skey=None, rkey=None, roff=None, rwidth=1):
            si = names_s.get(skey or key)
            ri = names_r.get(rkey or key, rwidth)
            if roff is not None:
                ri = ri + roff
            return pltpu.make_async_remote_copy(
                src_ref=src, dst_ref=dst, send_sem=ssem.at[si], recv_sem=rsem.at[ri],
                device_id=devs[to], device_id_type=MESH,
            )

        def local(key, src, dst):
            return pltpu.make_async_copy(src, dst, lsem.at[names_l.get(key)])

        def slot(z_, k_):
            return pl.ds(pl.multiple_of((z_ * 2 + k_) * TOK, TOK), TOK)

        def part(z_, k_, lo):
            return pl.ds(pl.multiple_of((z_ * 2 + k_) * TOK + lo, 64), 64)

        def cols(group_y, group_z):
            return pl.ds(pl.multiple_of((group_y * 4 + group_z) * WID, 128), WID)

        peers = [partner, devs["x+"], devs["x-"], devs["y+"], devs["y-"], devs["y2"],
                 devs["z+0"], devs["z+1"], devs["z-0"], devs["z-1"]]
        barrier = pltpu.get_barrier_semaphore()
        for peer in peers:
            pl.semaphore_signal(barrier, inc=1, device_id=peer, device_id_type=MESH)
        pl.semaphore_wait(barrier, len(peers))

        d = [(y + 4 - (2 * k + j)) % 4 for j in (0, 1)]
        tok2 = tok_hbm

        t_own = local("t", tok2, tok_v.at[slot(z, k)])
        T0 = remote("T0", tok2, tok_v.at[slot(z, k)], "z+")
        T1 = remote("T1", tok2, tok_v.at[slot(z, k)], "z-")
        T2 = remote("T2", tok2, tok_v.at[slot(z, k)], "p")
        T0r = remote("T0", tok2, tok_v.at[slot(zm, k)], "z+")
        T1r = remote("T1", tok2, tok_v.at[slot(zp, k)], "z-")
        T2r = remote("T2", tok2, tok_v.at[slot(z, kk)], "p")
        T3 = remote("T3", tok_v.at[slot(zm, k)], tok_v.at[slot(zm, k)], "p")
        T4 = remote("T4", tok_v.at[slot(zp, k)], tok_v.at[slot(zp, k)], "p")
        T3r = remote("T3", tok_v.at[slot(zm, kk)], tok_v.at[slot(zm, kk)], "p")
        T4r = remote("T4", tok_v.at[slot(zp, kk)], tok_v.at[slot(zp, kk)], "p")
        T5 = remote("T5", tok_v.at[part(zm, k, 0)], tok_v.at[part(zm, k, 0)], "z+")
        T6 = remote("T6", tok_v.at[part(zp, k, 64)], tok_v.at[part(zp, k, 64)], "z-")
        T5r = remote("T5", tok_v.at[part(zo, k, 0)], tok_v.at[part(zo, k, 0)], "z+")
        T6r = remote("T6", tok_v.at[part(zo, k, 64)], tok_v.at[part(zo, k, 64)], "z-")
        T7 = remote("T7", tok_v.at[part(zo, k, 0)], tok_v.at[part(zo, k, 0)], "p")
        T8 = remote("T8", tok_v.at[part(zo, k, 64)], tok_v.at[part(zo, k, 64)], "p")
        T7r = remote("T7", tok_v.at[part(zo, kk, 0)], tok_v.at[part(zo, kk, 0)], "p")
        T8r = remote("T8", tok_v.at[part(zo, kk, 64)], tok_v.at[part(zo, kk, 64)], "p")

        def cot(group_y, group_z):
            return cot_hbm.at[:, cols(group_y, group_z)]

        c_own = [local(f"c{j}", cot(2 * k + j, z), cb.at[j, slot(z, k)]) for j in (0, 1)]
        c_sends = []
        for j in (0, 1):
            row = []
            for k_ in (0, 1):
                row.append(remote(f"C1{j}{k_}", cot(2 * k_ + j, zp), cb.at[j, slot(z, k)], f"z+{k_}",
                                  rkey=f"C1r{j}", roff=k, rwidth=2))
                row.append(remote(f"C2{j}{k_}", cot(2 * k_ + j, zm), cb.at[j, slot(z, k)], f"z-{k_}",
                                  rkey=f"C2r{j}", roff=k, rwidth=2))
            row.append(remote(f"C3{j}", cot(j, zo), crel.at[0, j], "z+"))
            row.append(remote(f"C4{j}", cot(2 + j, zo), crel.at[1, j], "z-"))
            row.append(remote(f"C0{j}", cot(2 * kk + j, z), cb.at[j, slot(z, k)], "p"))
            c_sends.append(row)
        C3r = [remote(f"C3{j}", cot(j, zo), crel.at[0, j], "z+") for j in (0, 1)]
        C4r = [remote(f"C4{j}", cot(2 + j, zo), crel.at[1, j], "z-") for j in (0, 1)]
        C5 = [remote(f"C5{j}", crel.at[0, j], cb.at[j, slot(zm, k)], "z+0", rkey=f"C5r{j}", roff=k, rwidth=2) for j in (0, 1)]
        C6 = [remote(f"C6{j}", crel.at[1, j], cb.at[j, slot(zp, k)], "z-1", rkey=f"C5r{j}", roff=k, rwidth=2) for j in (0, 1)]

        def c_recvs(j):
            out = [remote(f"C0{j}", cot(j, z), cb.at[j, slot(z, kk)], "p")]
            for i in (0, 1):
                out.append(remote(f"C1{j}0", cot(j, z), cb.at[j, slot(zm, i)], "z+", rkey=f"C1r{j}", roff=i, rwidth=2))
                out.append(remote(f"C2{j}0", cot(j, z), cb.at[j, slot(zp, i)], "z-", rkey=f"C2r{j}", roff=i, rwidth=2))
                out.append(remote(f"C5{j}", cot(j, z), cb.at[j, slot(zo, i)], "z+", rkey=f"C5r{j}", roff=i, rwidth=2))
            return out

        def wq(j, q):
            return wc_hbm.at[j, pl.ds(q * QTR, QTR)]

        def wlo(j, q):
            return wc_hbm.at[j, pl.ds(q * QTR, HALF)]

        def whi(j, q):
            return wc_hbm.at[j, pl.ds(q * QTR + HALF, HALF)]

        q_mine = q_hbm.at[pl.ds(x * QTR, QTR)]
        W0 = [remote(f"W0{j}", q_mine, wq(j, x), "y+") for j in (0, 1)]
        W1 = [remote(f"W1{j}", q_mine, wq(j, x), "y-") for j in (0, 1)]
        W2 = [remote(f"W2{j}", wlo(j, x), wlo(j, x), "y+") for j in (0, 1)]
        W3 = [remote(f"W3{j}", whi(j, x), whi(j, x), "y-") for j in (0, 1)]
        W4 = [remote(f"W4{j}", wq(j, x), wq(j, x), "x+") for j in (0, 1)]
        W5 = [remote(f"W5{j}", wq(j, x), wq(j, x), "x-") for j in (0, 1)]
        W4r = [remote(f"W4{j}", wq(j, xm), wq(j, xm), "x+") for j in (0, 1)]
        W5r = [remote(f"W5{j}", wq(j, xp), wq(j, xp), "x-") for j in (0, 1)]
        W6 = [remote(f"W6{j}", wlo(j, xm), wlo(j, xm), "x+") for j in (0, 1)]
        W7 = [remote(f"W7{j}", whi(j, xp), whi(j, xp), "x-") for j in (0, 1)]
        W6r = [remote(f"W6{j}", wlo(j, xo), wlo(j, xo), "x+") for j in (0, 1)]
        W7r = [remote(f"W7{j}", whi(j, xo), whi(j, xo), "x-") for j in (0, 1)]
        V = [[remote(f"V{j}{i}", tab_hbm, tabv.at[j], to) for i, to in enumerate(("y+", "y-", "y2"))] for j in (0, 1)]

        def tab_start():
            for j in (0, 1):
                @pl.when(d[j] == 0)
                def _(j=j):
                    for copy in V[j]:
                        copy.start()
                    local(f"v{j}", tab_hbm, tabv.at[j]).start()

        def tab_finish():
            for j in (0, 1):
                @pl.when(d[j] == 0)
                def _(j=j):
                    local(f"v{j}", tab_hbm, tabv.at[j]).wait()

                for i, dist in enumerate((1, 3, 2)):
                    @pl.when(d[j] == dist)
                    def _(j=j, i=i):
                        V[j][i].wait_recv()
            cp = local("tab", tabv, tabs)
            cp.start()
            cp.wait()

        def w_first():
            for j in (0, 1):
                @pl.when(d[j] == 0)
                def _(j=j):
                    W0[j].start()
                    W1[j].start()

        def w_second():
            for j in (0, 1):
                @pl.when(d[j] == 1)
                def _(j=j):
                    W0[j].wait_recv()
                    W2[j].start()
                    W4[j].start()
                    W5[j].start()

                @pl.when(d[j] == 3)
                def _(j=j):
                    W1[j].wait_recv()
                    W3[j].start()
                    W4[j].start()
                    W5[j].start()

        def w_third():
            for j in (0, 1):
                @pl.when(d[j] == 2)
                def _(j=j):
                    W2[j].wait_recv()
                    W3[j].wait_recv()
                    W4[j].start()
                    W5[j].start()

        def w_fourth():
            for j in (0, 1):
                @pl.when(d[j] != 0)
                def _(j=j):
                    W4r[j].wait_recv()
                    W6[j].start()
                    W5r[j].wait_recv()
                    W7[j].start()

        def w_load(j):
            @pl.when(d[j] != 0)
            def _():
                W6r[j].wait_recv()
                W7r[j].wait_recv()
                cp = local("w", wc_hbm.at[j], wst.at[pl.ds(0, NSLOT)])
                cp.start()
                cp.wait()

            @pl.when(d[j] == 0)
            def _():
                cp = local("w", q_hbm, wst.at[pl.ds(0, NSLOT)])
                cp.start()
                cp.wait()

        def grads(j):
            @pl.loop(0, 16)
            def _(r):
                rows = pl.ds(pl.multiple_of(r * 256, 256), 256)
                g = lax.dot_general(tok_v[:, rows], cb[j], (((0,), (0,)), ((), ())), preferred_element_type=F32)
                g = g.astype(BF16)
                for h in (0, 1):
                    for c in range(COLS):
                        gw[(r * 2 + h) * COLS + c] = g[h * BS:(h + 1) * BS, c * BS:(c + 1) * BS]

        def pick(j):
            for o in range(OWN):
                @pl.loop(0, SLOTS)
                def _(s, o=o):
                    gs[j, o, s] = gw[tabs[j, 2 + o // 4, (o % 4) * 32 + s]]

        def assemble(j):
            @pl.loop(0, ROWS)
            def _(r):
                for c in range(COLS):
                    gw[r * COLS + c] = wst[tabs[j, r // 16, (r % 16) * 8 + c]]

        def forward(j):
            @pl.loop(0, 4)
            def _(m):
                rows = pl.ds(pl.multiple_of(m * 256, 256), 256)
                w = jnp.concatenate(
                    [jnp.concatenate([gw[r * COLS + c] for c in range(COLS)], axis=1) for r in range(ROWS)], axis=0
                )
                o = jnp.dot(tok_v[rows, :], w, preferred_element_type=F32)
                ob[j, rows, :] = o.astype(BF16)

        o_own = [local(f"o{j}", ob.at[j, slot(z, k)], out_hbm.at[:, cols(2 * k + j, z)]) for j in (0, 1)]
        o_sends = []
        for j in (0, 1):
            dst = out_hbm.at[:, cols(2 * k + j, z)]
            row = []
            row.append(remote(f"O3{j}", ob.at[j, slot(zo, 0)], orel.at[0, j], "z+"))
            row.append(remote(f"O4{j}", ob.at[j, slot(zo, 1)], orel.at[1, j], "z-"))
            for i in (0, 1):
                row.append(remote(f"O1{j}{i}", ob.at[j, slot(zp, i)], dst, f"z+{i}", rkey=f"O1r{j}", roff=k, rwidth=2))
                row.append(remote(f"O2{j}{i}", ob.at[j, slot(zm, i)], dst, f"z-{i}", rkey=f"O2r{j}", roff=k, rwidth=2))
            row.append(remote(f"O0{j}", ob.at[j, slot(z, kk)], dst, "p"))
            o_sends.append(row)
        O3r = [remote(f"O3{j}", orel.at[0, j], orel.at[0, j], "z+") for j in (0, 1)]
        O4r = [remote(f"O4{j}", orel.at[1, j], orel.at[1, j], "z-") for j in (0, 1)]
        O5 = [remote(f"O5{j}", orel.at[0, j], out_hbm.at[:, cols(2 * k + j, zm)], "z+0", rkey=f"O5r{j}", roff=k, rwidth=2) for j in (0, 1)]
        O6 = [remote(f"O6{j}", orel.at[1, j], out_hbm.at[:, cols(2 * k + j, zp)], "z-1", rkey=f"O5r{j}", roff=k, rwidth=2) for j in (0, 1)]

        def o_recvs(j):
            src = ob.at[j, slot(z, 0)]
            out = [remote(f"O0{j}", src, out_hbm.at[:, cols(2 * kk + j, z)], "p")]
            for i in (0, 1):
                out.append(remote(f"O1{j}0", src, out_hbm.at[:, cols(2 * i + j, zm)], "z+", rkey=f"O1r{j}", roff=i, rwidth=2))
                out.append(remote(f"O2{j}0", src, out_hbm.at[:, cols(2 * i + j, zp)], "z-", rkey=f"O2r{j}", roff=i, rwidth=2))
                out.append(remote(f"O5{j}", src, out_hbm.at[:, cols(2 * i + j, zo)], "z+", rkey=f"O5r{j}", roff=i, rwidth=2))
            return out

        def add1(dst, src, n):
            @pl.loop(0, n)
            def _(i):
                dst[i] = (dst[i].astype(F32) + src[i].astype(F32)).astype(BF16)

        def add2(dst, a, b, n):
            @pl.loop(0, n)
            def _(i):
                dst[i] = (dst[i].astype(F32) + a[i].astype(F32) + b[i].astype(F32)).astype(BF16)

        def sum3(out, dst, a, b, n):
            @pl.loop(0, n)
            def _(i):
                out[i] = dst[i].astype(F32) + a[i].astype(F32) + b[i].astype(F32)

        lo, hi = pl.ds(0, LO), pl.ds(LO, HI)

        class XStage:
            def __init__(self, name, j, base, first, second):
                self.j, self.base = j, base
                self.first, self.second = first, second
                self.c0 = remote(f"{name}0", gs.at[j, base + xo, lo], first.at[0], "x+")
                self.c1 = remote(f"{name}1", gs.at[j, base + xo, hi], first.at[1, pl.ds(0, HI)], "x-")
                self.c2 = remote(f"{name}2", gs.at[j, base + xp], second.at[0], "x+")
                self.c3 = remote(f"{name}3", gs.at[j, base + xm], second.at[1], "x-")

            def start(self):
                self.c0.start()
                self.c1.start()

            def middle(self):
                self.c0.wait_recv()
                add1(gs.at[self.j, self.base + xp, lo], self.first.at[0], LO)
                self.c2.start()
                self.c1.wait_recv()
                add1(gs.at[self.j, self.base + xm, hi], self.first.at[1], HI)
                self.c3.start()

            def arrive(self):
                self.c2.wait_recv()
                self.c3.wait_recv()

            def sends(self):
                return [self.c0, self.c1, self.c2, self.c3]

        class YStage:
            def __init__(self, name, j, whole, low, high, low_dst, high_dst, second):
                self.j = j
                self.c0 = remote(f"{name}0", low, low_dst, "y+")
                self.c1 = remote(f"{name}1", high, high_dst, "y-")
                self.c2 = remote(f"{name}2", whole, second.at[0], "y+")
                self.c3 = remote(f"{name}3", whole, second.at[1], "y-")
                self.low, self.high, self.low_dst, self.high_dst = low, high, low_dst, high_dst

            def start(self):
                @pl.when(d[self.j] == 2)
                def _():
                    self.c0.start()
                    self.c1.start()

            def middle(self, n_low, n_high):
                @pl.when(d[self.j] == 3)
                def _():
                    self.c0.wait_recv()
                    add1(self.low, self.low_dst, n_low)
                    self.c2.start()

                @pl.when(d[self.j] == 1)
                def _():
                    self.c1.wait_recv()
                    add1(self.high, self.high_dst, n_high)
                    self.c3.start()

            def arrive(self):
                self.c2.wait_recv()
                self.c3.wait_recv()

            def wait_sends(self):
                @pl.when(d[self.j] == 2)
                def _():
                    self.c0.wait_send()
                    self.c1.wait_send()

                @pl.when(d[self.j] == 3)
                def _():
                    self.c2.wait_send()

                @pl.when(d[self.j] == 1)
                def _():
                    self.c3.wait_send()

        AX = [XStage(f"A{j}", j, 0, ra1.at[j], ra2.at[j]) for j in (0, 1)]
        AY = [YStage(f"Y{j}", j, gs.at[j, x], gs.at[j, x, lo], gs.at[j, x, hi], ry1, ry1.at[pl.ds(0, HI)], ry2) for j in (0, 1)]
        gs84 = [gs.at[j, pl.ds(4, 4)] for j in (0, 1)]
        BY = [YStage(f"Z{j}", j, gs84[j], gs.at[j, pl.ds(4, 2)], gs.at[j, pl.ds(6, 2)], rz1, rz1, rz2) for j in (0, 1)]
        BX = [XStage(f"B{j}", j, 4, rb1, rb2) for j in (0, 1)]

        def ax_end(j):
            AX[j].arrive()
            add2(gs.at[j, x], ra2.at[j, 0], ra2.at[j, 1], SLOTS)
            AY[j].start()

        def add_nested(dst, srcs, n):
            for o in range(n):
                if len(srcs) == 1:
                    add1(dst.at[o], srcs[0].at[o], SLOTS)
                else:
                    add2(dst.at[o], srcs[0].at[o], srcs[1].at[o], SLOTS)

        def by_middle(j):
            s = BY[j]

            @pl.when(d[j] == 3)
            def _():
                s.c0.wait_recv()
                add_nested(s.low, [rz1], 2)
                s.c2.start()

            @pl.when(d[j] == 1)
            def _():
                s.c1.wait_recv()
                add_nested(s.high, [rz1], 2)
                s.c3.start()

        def by_end(j):
            @pl.when(d[j] == 0)
            def _():
                BY[j].arrive()
                add_nested(gs84[j], [rz2.at[0], rz2.at[1]], 4)
                BX[j].start()

        def bx_middle(j):
            @pl.when(d[j] == 0)
            def _():
                BX[j].middle()

        g_own = local("g", fin.at[k], wg_hbm)
        G = remote("G", fin.at[kk], wg_hbm, "p")

        def finals(j):
            @pl.when(d[j] == 0)
            def _():
                AY[j].arrive()
                sum3(fin.at[0], gs.at[j, x], ry2.at[0], ry2.at[1], SLOTS)
                BX[j].arrive()
                sum3(fin.at[1], gs.at[j, 4 + x], rb2.at[0], rb2.at[1], SLOTS)
                G.start()
                g_own.start()

        t_own.start()
        for copy in (T0, T1, T2):
            copy.start()
        tab_start()
        w_first()
        for copy in c_own:
            copy.start()
        for copy in c_sends[0]:
            copy.start()
        wst[NSLOT] = jnp.zeros((BS, BS), BF16)
        tab_finish()
        w_second()
        w_third()
        T0r.wait_recv()
        T5.start()
        T3.start()
        T1r.wait_recv()
        T6.start()
        T4.start()
        for copy in c_sends[1]:
            copy.start()
        C3r[0].wait_recv()
        C5[0].start()
        C4r[0].wait_recv()
        C6[0].start()
        T5r.wait_recv()
        T7.start()
        T6r.wait_recv()
        T8.start()
        t_own.wait()
        for copy in (T2r, T3r, T4r, T7r, T8r):
            copy.wait_recv()
        c_own[0].wait()
        for copy in c_recvs(0):
            copy.wait_recv()
        grads(0)
        pick(0)
        AX[0].start()
        BY[0].start()
        C3r[1].wait_recv()
        C5[1].start()
        C4r[1].wait_recv()
        C6[1].start()
        w_fourth()
        c_own[1].wait()
        for copy in c_recvs(1):
            copy.wait_recv()
        grads(1)
        pick(1)
        AX[1].start()
        BY[1].start()
        AX[0].middle()
        by_middle(0)
        w_load(0)
        assemble(0)
        forward(0)
        o_own[0].start()
        for copy in o_sends[0]:
            copy.start()
        AX[1].middle()
        by_middle(1)
        ax_end(0)
        w_load(1)
        assemble(1)
        forward(1)
        o_own[1].start()
        for copy in o_sends[1]:
            copy.start()
        by_end(0)
        by_end(1)
        ax_end(1)
        AY[0].middle(LO, HI)
        AY[1].middle(LO, HI)
        O3r[0].wait_recv()
        O5[0].start()
        O4r[0].wait_recv()
        O6[0].start()
        bx_middle(0)
        bx_middle(1)
        O3r[1].wait_recv()
        O5[1].start()
        O4r[1].wait_recv()
        O6[1].start()
        finals(0)
        finals(1)

        for j in (0, 1):
            for copy in o_recvs(j):
                copy.wait_recv()
            o_own[j].wait()

        own_final = (y // 2) == k

        @pl.when(own_final)
        def _():
            g_own.wait()
            G.wait_send()

        @pl.when(jnp.logical_not(own_final))
        def _():
            G.wait_recv()

        for copy in (T0, T1, T2, T3, T4, T5, T6, T7, T8):
            copy.wait_send()
        for j in (0, 1):
            for copy in c_sends[j] + [C5[j], C6[j]] + o_sends[j] + [O5[j], O6[j]] + AX[j].sends():
                copy.wait_send()
            AY[j].wait_sends()
            BY[j].wait_sends()

            @pl.when(d[j] == 0)
            def _(j=j):
                for copy in [W0[j], W1[j]] + V[j] + BX[j].sends():
                    copy.wait_send()

            @pl.when(d[j] == 1)
            def _(j=j):
                W2[j].wait_send()

            @pl.when(d[j] == 3)
            def _(j=j):
                W3[j].wait_send()

            @pl.when(d[j] != 0)
            def _(j=j):
                for copy in (W4[j], W5[j], W6[j], W7[j]):
                    copy.wait_send()

    return kernel


def tables(slot_ids):
    numbers = jnp.arange(ROWS * 8, dtype=jnp.int32)
    block = jnp.where(numbers % 8 < COLS, (numbers // 8) * COLS + numbers % 8, -1)
    match = (slot_ids[:, None] == block[None, :]).astype(jnp.int32)
    index = jnp.sum(match * (jnp.arange(NSLOT, dtype=jnp.int32)[:, None] - NSLOT), axis=0) + NSLOT
    pad = ((0, 0), (0, 32 - SLOTS))
    ids = slot_ids.reshape(OWN, SLOTS)
    ids = jnp.pad(ids, pad).reshape(2, 128)
    return jnp.concatenate([index.reshape(2, 128), ids, jnp.zeros((4, 128), jnp.int32)], axis=0)


def shards(tokens, cotangent, master, block_ids, live_count):
    owners, slots = block_ids.shape
    live_mask = (jnp.arange(slots, dtype=jnp.int32)[None, :] < live_count).astype(jnp.float32)
    quantized = fake_quant(master, live_mask).reshape(owners * slots, BS, BS)
    table = tables(block_ids.reshape(owners * slots))
    vmem = pltpu.VMEM
    blk = (BS, BS)
    anyspec = pl.BlockSpec(memory_space=pl.ANY)
    outputs, w_grad, _ = pl.pallas_call(
        make_kernel(Names(), Names(), Names()),
        out_shape=(
            jax.ShapeDtypeStruct(cotangent.shape, BF16),
            jax.ShapeDtypeStruct((slots,) + blk, F32),
            jax.ShapeDtypeStruct((2, NSLOT) + blk, BF16),
        ),
        in_specs=[anyspec] * 4,
        out_specs=(anyspec,) * 3,
        scratch_shapes=[
            vmem((8 * TOK, ROWS * BS), BF16),
            vmem((2, 8 * TOK, WID), BF16),
            vmem((2, 2, TOK, WID), BF16),
            vmem((ROWS * COLS,) + blk, BF16),
            vmem((NSLOT + 1,) + blk, BF16),
            vmem((2, 8 * TOK, WID), BF16),
            vmem((2, 2, TOK, WID), BF16),
            vmem((2, OWN, SLOTS) + blk, BF16),
            vmem((2, 2, LO) + blk, BF16),
            vmem((2, 2, SLOTS) + blk, BF16),
            vmem((LO,) + blk, BF16),
            vmem((2, SLOTS) + blk, BF16),
            vmem((2, SLOTS) + blk, BF16),
            vmem((2, 4, SLOTS) + blk, BF16),
            vmem((2, LO) + blk, BF16),
            vmem((2, SLOTS) + blk, BF16),
            vmem((2, SLOTS) + blk, F32),
            vmem((2, 8, 128), jnp.int32),
            pltpu.SMEM((2, 8, 128), jnp.int32),
            pltpu.SemaphoreType.DMA((112,)),
            pltpu.SemaphoreType.DMA((112,)),
            pltpu.SemaphoreType.DMA((16,)),
        ],
        compiler_params=pltpu.CompilerParams(
            collective_id=0, has_side_effects=True, vmem_limit_bytes=66 * 1024 * 1000
        ),
    )(tokens, cotangent, quantized, table)
    owner = lax.axis_index("dp") * lax.axis_size("seq") + lax.axis_index("seq")
    count = lax.dynamic_slice(live_count, (owner, 0), (1, 1))
    mine = jnp.arange(slots, dtype=jnp.int32)[None, :, None, None] < count[:, :, None, None]
    return (outputs, jnp.where(mine, w_grad[None], 0.0))


def solution(mesh):
    return jax.shard_map(
        shards,
        mesh=mesh,
        in_specs=(
            P(("dp", "seq", "tensor"), None),
            P(("dp", "seq", "tensor"), None),
            P(None, "tensor", None, None),
            P(None, "tensor"),
            P(None, "tensor"),
        ),
        out_specs=(P(("dp", "seq", "tensor"), None), P(("dp", "seq"), "tensor", None, None)),
        check_vma=False,
    )
```

time: 371 us -> 223 us (0.60)
  Pallas kernels: 0 us -> 200 us
  waiting for transfers between devices: 130 us -> 0 us
  local copies, waits for them, and re-layouts: 94.1 us -> 5.68 us
  blocking collectives: 53.3 us -> 0 us
  matrix products: 44.3 us -> 0 us
  between operations: 14.1 us -> 0.68 us
  other arithmetic: 25.1 us -> 16 us
  starting transfers between devices: 7.92 us -> 0 us
    pallas_call x0 -> x1, Pallas kernels: none -> 200 us  [shards(): pl.pallas_call(make_kernel(Names(), Names(), Names()), out_shape=(jax.Sha...]
    all_gather x1 -> x0, waiting for transfers between devices: 71.8 us -> none  [shards(): gathered = lax.all_gather(tokens, 'tensor', axis=0, tiled=True)]
    all_to_all x1 -> x0, waiting for transfers between devices: 54.9 us -> none  [shards(): lax.all_to_all(cotangent, 'tensor', split_axis=1, concat_axis=0, tiled=True)]
    all_to_all x1 -> x0, blocking collectives: 53.3 us -> none  [shards(): lax.all_to_all(results.astype(jnp.bfloat16), 'tensor', split_axis=0, conc...]
    dot_general x2 -> x0, matrix products: 44.3 us -> none  [the longest x1 23.3 us: dense_gradient(): lax.dot_general(token_rows, grad_rows, (((0,), (0,)), ((), ())), preferre...]
    gather x2 -> x0, local copies, waits for them, and re-layouts: 26.6 us -> none  [the longest x1 15.5 us: pick_blocks(): return jnp.take(grid_blocks, slot_ids, axis=0)]
    dot_general x1 -> x0, local copies, waits for them, and re-layouts: 22.5 us -> none  [dense_gradient(): lax.dot_general(token_rows, grad_rows, (((0,), (0,)), ((), ())), preferre...]
    mul x1 -> x0, other arithmetic: 14.1 us -> none  [shards(): partial_value * live_mask.reshape(owners * slots)[:, None, None]]
  transfers between devices with their start and end apart: 3 -> 0, of which waited for: 3 -> 0; matrix products, arithmetic and copies ran while one was open for 24% -> 0% of each run, Pallas kernels for 0% -> 0%
where the time goes in v1:
time: 223 us
  Pallas kernels  200 us (90%)
  other arithmetic  16 us (7%)
  local copies, waits for them, and re-layouts  5.68 us (3%)
    pallas_call x1, Pallas kernels, shards(): pl.pallas_call(make_kernel(Names(), Names(), Names()), out_shape=(jax.Sha...  200 us
    convert_element_type x1, other arithmetic, fake_quant(): (levels * (block_peak / 7.0) * live_mask[..., None, None]).astype(jnp.bfl...  7.35 us

profile of v1, /device:TPU:9, one launch (start us, length us, event | category | flops | bytes accessed | tf_op | source)
XLA Modules:
  0.0 222.8 jit_solution(6012473177292825442)
XLA Ops:
  0.6 0.0 copy-start
  0.6 0.7 fusion.6
  1.4 3.9 %fusion = f32[8,21]{1,0:T(8,128)S(1)} fusion(bf16[8,21,128,128]{3,2,1,0:T(8,128)(2,1)} %param.7), kind=kLoop, calls=%fused_computation.2 | loop fusion | flops 8257368 | bytes 5505696 | tf_op jit(solution)/shard_map/reduce_max | solution.py:40
  5.3 7.4 %fusion.5 = bf16[8,21,128,128]{3,2,1,0:T(8,128)(2,1)} fusion(bf16[8,21,128,128]{3,2,1,0:T(8,128)(2,1)} %param.7, f32[8,21]{1,0:T(8,128)S(1)} %fusion.6, f32[8,21]{1,0:T(8,128)S(1)} %get-tuple-element.7, f32[8,21]{1,0:T(8,128)S(1)} %get-tuple-element.6), kind=kLoop, calls=%fused_computation.7 | loop fusion | flops 19267584 | bytes 11012064 | tf_op jit(solution)/shard_map/convert_element_type | solution.py:42
  12.6 0.0 copy-done
  12.6 0.1 reshape.89
  12.7 0.1 eq.18
  12.8 0.1 select_reduce_fusion
  12.9 0.1 pad.7.clone
  13.0 0.7 add_add_fusion.tab_hbm
  13.7 200.4 %shard_map.71 = (bf16[128,14336]{1,0:T(8,128)(2,1)}, f32[21,128,128]{2,1,0:T(8,128)}, bf16[2,168,128,128]{3,2,1,0:T(8,128)(2,1)}) custom-call(bf16[128,4096]{1,0:T(8,128)(2,1)} %tok_hbm.1, bf16[128,14336]{1,0:T(8,128)(2,1)} %cot_hbm.1, bf16[168,128,128]{2,1,0:T(8,128)(2,1)} %bitcast.7, s32[8,128]{1,0:T(8,128)} %add_add_fusion.tab_hbm), custom_call_target="tpu_custom_call" | custom-call | tf_op jit(solution)/shard_map/pallas_call | solution.py:615
  214.1 1.2 constant_dynamic-slice_fusion
  215.3 0.6 iota_compare_fusion.1
  216.0 2.6 %select_bitcast_fusion = f32[1,21,128,128]{3,2,1,0:T(8,128)} fusion(f32[21,128,128]{2,1,0:T(8,128)} %get-tuple-element.5, pred[21]{0:T(512)(128)(4,1)S(1)} %iota_compare_fusion.1), kind=kLoop, calls=%fused_computation.8 | loop fusion | flops 344064 | bytes 2752533 | tf_op jit(solution)/shard_map/jit(_where)/select_n | solution.py:655
  218.6 4.2 %copy.8 = bf16[128,14336]{1,0:T(8,128)(2,1)} copy(bf16[128,14336]{1,0:T(8,128)(2,1)} %get-tuple-element.10) | data formatting | bytes 7340032
  (6 shorter events, 0.0 us)
Async XLA Ops:
  0.6 12.0 %copy-start = (s32[8,21]{1,0:T(8,128)S(1)}, s32[8,21]{1,0:T(8,128)}, u32[]{:S(2)}) copy-start(s32[8,21]{1,0:T(8,128)} %param.8) | copy-start | bytes 2020

commit v2 on v1

--- a/solution.py
+++ b/solution.py
@@ -13,8 +13,11 @@
 OWN = 8
 SLOTS = 21
 NSLOT = OWN * SLOTS
-QTR = NSLOT // 4
+QTR = 28
 HALF = QTR // 2
+YLO = 4 * QTR
+YN = NSLOT - YLO
+YH = YN // 2
 LO, HI = 11, 10
 WID = COLS * BS
 TOK = 128
@@ -33,13 +36,6 @@
             self.at[key] = self.n
             self.n += width
         return self.at[key]
-
-
-def fake_quant(master, live_mask):
-    master_wide = master.astype(jnp.float32)
-    block_peak = jnp.max(jnp.abs(master_wide), axis=(-2, -1), keepdims=True) + 1e-06
-    levels = jnp.floor(master_wide * (7.0 / block_peak) + 0.5)
-    return (levels * (block_peak / 7.0) * live_mask[..., None, None]).astype(jnp.bfloat16)
 
 
 def make_kernel(names_s, names_r, names_l):
@@ -131,13 +127,13 @@
         c_sends = []
         for j in (0, 1):
             row = []
+            row.append(remote(f"C3{j}", cot(j, zo), crel.at[0, j], "z+"))
+            row.append(remote(f"C4{j}", cot(2 + j, zo), crel.at[1, j], "z-"))
             for k_ in (0, 1):
                 row.append(remote(f"C1{j}{k_}", cot(2 * k_ + j, zp), cb.at[j, slot(z, k)], f"z+{k_}",
                                   rkey=f"C1r{j}", roff=k, rwidth=2))
                 row.append(remote(f"C2{j}{k_}", cot(2 * k_ + j, zm), cb.at[j, slot(z, k)], f"z-{k_}",
                                   rkey=f"C2r{j}", roff=k, rwidth=2))
-            row.append(remote(f"C3{j}", cot(j, zo), crel.at[0, j], "z+"))
-            row.append(remote(f"C4{j}", cot(2 + j, zo), crel.at[1, j], "z-"))
             row.append(remote(f"C0{j}", cot(2 * kk + j, z), cb.at[j, slot(z, k)], "p"))
             c_sends.append(row)
         C3r = [remote(f"C3{j}", cot(j, zo), crel.at[0, j], "z+") for j in (0, 1)]
@@ -162,19 +158,26 @@
         def whi(j, q):
             return wc_hbm.at[j, pl.ds(q * QTR + HALF, HALF)]
 
-        q_mine = q_hbm.at[pl.ds(x * QTR, QTR)]
-        W0 = [remote(f"W0{j}", q_mine, wq(j, x), "y+") for j in (0, 1)]
-        W1 = [remote(f"W1{j}", q_mine, wq(j, x), "y-") for j in (0, 1)]
-        W2 = [remote(f"W2{j}", wlo(j, x), wlo(j, x), "y+") for j in (0, 1)]
-        W3 = [remote(f"W3{j}", whi(j, x), whi(j, x), "y-") for j in (0, 1)]
-        W4 = [remote(f"W4{j}", wq(j, x), wq(j, x), "x+") for j in (0, 1)]
-        W5 = [remote(f"W5{j}", wq(j, x), wq(j, x), "x-") for j in (0, 1)]
-        W4r = [remote(f"W4{j}", wq(j, xm), wq(j, xm), "x+") for j in (0, 1)]
-        W5r = [remote(f"W5{j}", wq(j, xp), wq(j, xp), "x-") for j in (0, 1)]
-        W6 = [remote(f"W6{j}", wlo(j, xm), wlo(j, xm), "x+") for j in (0, 1)]
-        W7 = [remote(f"W7{j}", whi(j, xp), whi(j, xp), "x-") for j in (0, 1)]
-        W6r = [remote(f"W6{j}", wlo(j, xo), wlo(j, xo), "x+") for j in (0, 1)]
-        W7r = [remote(f"W7{j}", whi(j, xo), whi(j, xo), "x-") for j in (0, 1)]
+        def wu(j, lo=0, n=YN):
+            return wc_hbm.at[j, pl.ds(YLO + lo, n)]
+
+        JS = (0, 1)
+        W0 = [remote(f"W0{j}", wq(j, x), wq(j, x), "y+") for j in JS]
+        W1 = [remote(f"W1{j}", wq(j, x), wq(j, x), "y-") for j in JS]
+        W2 = [remote(f"W2{j}", wlo(j, x), wlo(j, x), "y+") for j in JS]
+        W3 = [remote(f"W3{j}", whi(j, x), whi(j, x), "y-") for j in JS]
+        W4 = [remote(f"W4{j}", wq(j, x), wq(j, x), "x+") for j in JS]
+        W5 = [remote(f"W5{j}", wq(j, x), wq(j, x), "x-") for j in JS]
+        W4r = [remote(f"W4{j}", wq(j, xm), wq(j, xm), "x+") for j in JS]
+        W5r = [remote(f"W5{j}", wq(j, xp), wq(j, xp), "x-") for j in JS]
+        W6 = [remote(f"W6{j}", wlo(j, xm), wlo(j, xm), "x+") for j in JS]
+        W7 = [remote(f"W7{j}", whi(j, xp), whi(j, xp), "x-") for j in JS]
+        W6r = [remote(f"W6{j}", wlo(j, xo), wlo(j, xo), "x+") for j in JS]
+        W7r = [remote(f"W7{j}", whi(j, xo), whi(j, xo), "x-") for j in JS]
+        U0 = [remote(f"WU0{j}", wu(j), wu(j), "y+") for j in JS]
+        U1 = [remote(f"WU1{j}", wu(j), wu(j), "y-") for j in JS]
+        U2 = [remote(f"WU2{j}", wu(j, 0, YH), wu(j, 0, YH), "y+") for j in JS]
+        U3 = [remote(f"WU3{j}", wu(j, YH, YH), wu(j, YH, YH), "y-") for j in JS]
         V = [[remote(f"V{j}{i}", tab_hbm, tabv.at[j], to) for i, to in enumerate(("y+", "y-", "y2"))] for j in (0, 1)]
 
         def tab_start():
@@ -199,12 +202,34 @@
             cp.start()
             cp.wait()
 
+        def quantize(j, start, n):
+            @pl.loop(0, n // 4)
+            def _(i):
+                rows = pl.ds(start + i * 4, 4)
+                wide = wst[rows].astype(F32)
+                peak = jnp.max(jnp.abs(wide), axis=(1, 2), keepdims=True) + 1e-06
+                levels = jnp.floor(wide * (7.0 / peak) + 0.5)
+                wst[rows] = (levels * (peak / 7.0)).astype(BF16)
+
+            cp = local("qw", wst.at[pl.ds(start, n)], wc_hbm.at[j, pl.ds(start, n)])
+            cp.start()
+            cp.wait()
+
         def w_first():
             for j in (0, 1):
                 @pl.when(d[j] == 0)
                 def _(j=j):
+                    cp = local("q", q_hbm, wst.at[pl.ds(0, NSLOT)])
+                    cp.start()
+                    cp.wait()
+                    quantize(j, x * QTR, QTR)
                     W0[j].start()
                     W1[j].start()
+                    quantize(j, YLO, YN)
+                    U0[j].start()
+                    U1[j].start()
+                    for q in (xp, xo, xm):
+                        quantize(j, q * QTR, QTR)
 
         def w_second():
             for j in (0, 1):
@@ -230,6 +255,18 @@
                     W3[j].wait_recv()
                     W4[j].start()
                     W5[j].start()
+
+        def w_relay():
+            for j in (0, 1):
+                @pl.when(d[j] == 1)
+                def _(j=j):
+                    U0[j].wait_recv()
+                    U2[j].start()
+
+                @pl.when(d[j] == 3)
+                def _(j=j):
+                    U1[j].wait_recv()
+                    U3[j].start()
 
         def w_fourth():
             for j in (0, 1):
@@ -245,15 +282,15 @@
             def _():
                 W6r[j].wait_recv()
                 W7r[j].wait_recv()
-                cp = local("w", wc_hbm.at[j], wst.at[pl.ds(0, NSLOT)])
-                cp.start()
-                cp.wait()
-
-            @pl.when(d[j] == 0)
+
+            @pl.when(d[j] == 2)
             def _():
-                cp = local("w", q_hbm, wst.at[pl.ds(0, NSLOT)])
-                cp.start()
-                cp.wait()
+                U2[j].wait_recv()
+                U3[j].wait_recv()
+
+            cp = local("w", wc_hbm.at[j], wst.at[pl.ds(0, NSLOT)])
+            cp.start()
+            cp.wait()
 
         def grads(j):
             @pl.loop(0, 16)
@@ -277,15 +314,21 @@
                 for c in range(COLS):
                     gw[r * COLS + c] = wst[tabs[j, r // 16, (r % 16) * 8 + c]]
 
-        def forward(j):
+        def forward(j, hooks):
             @pl.loop(0, 4)
             def _(m):
-                rows = pl.ds(pl.multiple_of(m * 256, 256), 256)
+                zz = (z + jnp.where(m == 0, 2, jnp.where(m == 1, 1, jnp.where(m == 2, 3, 0)))) % 4
+                rows = pl.ds(pl.multiple_of(zz * 256, 256), 256)
                 w = jnp.concatenate(
                     [jnp.concatenate([gw[r * COLS + c] for c in range(COLS)], axis=1) for r in range(ROWS)], axis=0
                 )
                 o = jnp.dot(tok_v[rows, :], w, preferred_element_type=F32)
                 ob[j, rows, :] = o.astype(BF16)
+                for at, steps in hooks.items():
+                    @pl.when(m == at)
+                    def _(steps=steps):
+                        for step in steps:
+                            step()
 
         o_own = [local(f"o{j}", ob.at[j, slot(z, k)], out_hbm.at[:, cols(2 * k + j, z)]) for j in (0, 1)]
         o_sends = []
@@ -296,6 +339,7 @@
             row.append(remote(f"O4{j}", ob.at[j, slot(zo, 1)], orel.at[1, j], "z-"))
             for i in (0, 1):
                 row.append(remote(f"O1{j}{i}", ob.at[j, slot(zp, i)], dst, f"z+{i}", rkey=f"O1r{j}", roff=k, rwidth=2))
+            for i in (0, 1):
                 row.append(remote(f"O2{j}{i}", ob.at[j, slot(zm, i)], dst, f"z-{i}", rkey=f"O2r{j}", roff=k, rwidth=2))
             row.append(remote(f"O0{j}", ob.at[j, slot(z, kk)], dst, "p"))
             o_sends.append(row)
@@ -333,39 +377,43 @@
         class XStage:
             def __init__(self, name, j, base, first, second):
                 self.j, self.base = j, base
-                self.first, self.second = first, second
+                self.first = first
                 self.c0 = remote(f"{name}0", gs.at[j, base + xo, lo], first.at[0], "x+")
                 self.c1 = remote(f"{name}1", gs.at[j, base + xo, hi], first.at[1, pl.ds(0, HI)], "x-")
-                self.c2 = remote(f"{name}2", gs.at[j, base + xp], second.at[0], "x+")
-                self.c3 = remote(f"{name}3", gs.at[j, base + xm], second.at[1], "x-")
+                self.c2l = remote(f"{name}2l", gs.at[j, base + xp, lo], second.at[0, lo], "x+")
+                self.c2h = remote(f"{name}2h", gs.at[j, base + xp, hi], second.at[0, hi], "x+")
+                self.c3l = remote(f"{name}3l", gs.at[j, base + xm, lo], second.at[1, lo], "x-")
+                self.c3h = remote(f"{name}3h", gs.at[j, base + xm, hi], second.at[1, hi], "x-")
 
             def start(self):
-                self.c0.start()
-                self.c1.start()
+                for copy in (self.c0, self.c1, self.c2h, self.c3l):
+                    copy.start()
 
             def middle(self):
                 self.c0.wait_recv()
                 add1(gs.at[self.j, self.base + xp, lo], self.first.at[0], LO)
-                self.c2.start()
+                self.c2l.start()
                 self.c1.wait_recv()
                 add1(gs.at[self.j, self.base + xm, hi], self.first.at[1], HI)
-                self.c3.start()
+                self.c3h.start()
 
             def arrive(self):
-                self.c2.wait_recv()
-                self.c3.wait_recv()
+                for copy in (self.c2h, self.c3l, self.c2l, self.c3h):
+                    copy.wait_recv()
 
             def sends(self):
-                return [self.c0, self.c1, self.c2, self.c3]
+                return [self.c0, self.c1, self.c2l, self.c2h, self.c3l, self.c3h]
 
         class YStage:
-            def __init__(self, name, j, whole, low, high, low_dst, high_dst, second):
-                self.j = j
-                self.c0 = remote(f"{name}0", low, low_dst, "y+")
-                self.c1 = remote(f"{name}1", high, high_dst, "y-")
-                self.c2 = remote(f"{name}2", whole, second.at[0], "y+")
-                self.c3 = remote(f"{name}3", whole, second.at[1], "y-")
-                self.low, self.high, self.low_dst, self.high_dst = low, high, low_dst, high_dst
+            def __init__(self, name, j, src, low, high, relay, high_relay, second, add):
+                self.j, self.add, self.relay = j, add, relay
+                self.low, self.high = src.at[low], src.at[high]
+                self.c0 = remote(f"{name}0", self.low, relay, "y+")
+                self.c1 = remote(f"{name}1", self.high, high_relay, "y-")
+                self.c2l = remote(f"{name}2l", self.low, second.at[0].at[low], "y+")
+                self.c2h = remote(f"{name}2h", self.high, second.at[0].at[high], "y+")
+                self.c3l = remote(f"{name}3l", self.low, second.at[1].at[low], "y-")
+                self.c3h = remote(f"{name}3h", self.high, second.at[1].at[high], "y-")
 
             def start(self):
                 @pl.when(d[self.j] == 2)
@@ -373,22 +421,30 @@
                     self.c0.start()
                     self.c1.start()
 
-            def middle(self, n_low, n_high):
+                @pl.when(d[self.j] == 3)
+                def _():
+                    self.c2h.start()
+
+                @pl.when(d[self.j] == 1)
+                def _():
+                    self.c3l.start()
+
+            def middle(self):
                 @pl.when(d[self.j] == 3)
                 def _():
                     self.c0.wait_recv()
-                    add1(self.low, self.low_dst, n_low)
-                    self.c2.start()
+                    self.add(self.low, self.relay, 0)
+                    self.c2l.start()
 
                 @pl.when(d[self.j] == 1)
                 def _():
                     self.c1.wait_recv()
-                    add1(self.high, self.high_dst, n_high)
-                    self.c3.start()
+                    self.add(self.high, self.relay, 1)
+                    self.c3h.start()
 
             def arrive(self):
-                self.c2.wait_recv()
-                self.c3.wait_recv()
+                for copy in (self.c2h, self.c3l, self.c2l, self.c3h):
+                    copy.wait_recv()
 
             def wait_sends(self):
                 @pl.when(d[self.j] == 2)
@@ -398,16 +454,25 @@
 
                 @pl.when(d[self.j] == 3)
                 def _():
-                    self.c2.wait_send()
+                    self.c2h.wait_send()
+                    self.c2l.wait_send()
 
                 @pl.when(d[self.j] == 1)
                 def _():
-                    self.c3.wait_send()
+                    self.c3l.wait_send()
+                    self.c3h.wait_send()
 
         AX = [XStage(f"A{j}", j, 0, ra1.at[j], ra2.at[j]) for j in (0, 1)]
-        AY = [YStage(f"Y{j}", j, gs.at[j, x], gs.at[j, x, lo], gs.at[j, x, hi], ry1, ry1.at[pl.ds(0, HI)], ry2) for j in (0, 1)]
+        def add_ay(dst, src, half):
+            add1(dst, src, (LO, HI)[half])
+
+        def add_by(dst, src, half):
+            for o in (0, 1):
+                add1(dst.at[o], src.at[o], SLOTS)
+
+        AY = [YStage(f"Y{j}", j, gs.at[j, x], lo, hi, ry1, ry1.at[pl.ds(0, HI)], ry2, add_ay) for j in (0, 1)]
         gs84 = [gs.at[j, pl.ds(4, 4)] for j in (0, 1)]
-        BY = [YStage(f"Z{j}", j, gs84[j], gs.at[j, pl.ds(4, 2)], gs.at[j, pl.ds(6, 2)], rz1, rz1, rz2) for j in (0, 1)]
+        BY = [YStage(f"Z{j}", j, gs84[j], pl.ds(0, 2), pl.ds(2, 2), rz1, rz1, rz2, add_by) for j in (0, 1)]
         BX = [XStage(f"B{j}", j, 4, rb1, rb2) for j in (0, 1)]
 
         def ax_end(j):
@@ -415,33 +480,12 @@
             add2(gs.at[j, x], ra2.at[j, 0], ra2.at[j, 1], SLOTS)
             AY[j].start()
 
-        def add_nested(dst, srcs, n):
-            for o in range(n):
-                if len(srcs) == 1:
-                    add1(dst.at[o], srcs[0].at[o], SLOTS)
-                else:
-                    add2(dst.at[o], srcs[0].at[o], srcs[1].at[o], SLOTS)
-
-        def by_middle(j):
-            s = BY[j]
-
-            @pl.when(d[j] == 3)
-            def _():
-                s.c0.wait_recv()
-                add_nested(s.low, [rz1], 2)
-                s.c2.start()
-
-            @pl.when(d[j] == 1)
-            def _():
-                s.c1.wait_recv()
-                add_nested(s.high, [rz1], 2)
-                s.c3.start()
-
         def by_end(j):
             @pl.when(d[j] == 0)
             def _():
                 BY[j].arrive()
-                add_nested(gs84[j], [rz2.at[0], rz2.at[1]], 4)
+                for o in range(4):
+                    add2(gs84[j].at[o], rz2.at[0, o], rz2.at[1, o], SLOTS)
                 BX[j].start()
 
         def bx_middle(j):
@@ -462,15 +506,41 @@
                 G.start()
                 g_own.start()
 
+        def o_start(j, *which):
+            def go():
+                for i in which:
+                    if i < 0:
+                        o_own[j].start()
+                    else:
+                        o_sends[j][i].start()
+            return go
+
+        def o_hooks(j):
+            return {0: [o_start(j, 0, 1)], 1: [o_start(j, 2, 3)], 2: [o_start(j, 4, 5)], 3: [o_start(j, 6, -1)]}
+
+        def o_relay(j):
+            O3r[j].wait_recv()
+            O5[j].start()
+            O4r[j].wait_recv()
+            O6[j].start()
+
+        def c_relay(j):
+            C3r[j].wait_recv()
+            C5[j].start()
+            C4r[j].wait_recv()
+            C6[j].start()
+
+        def reduce_start(j):
+            AX[j].start()
+            BY[j].start()
+
         t_own.start()
         for copy in (T0, T1, T2):
             copy.start()
         tab_start()
+        for copy in c_sends[0] + c_own:
+            copy.start()
         w_first()
-        for copy in c_own:
-            copy.start()
-        for copy in c_sends[0]:
-            copy.start()
         wst[NSLOT] = jnp.zeros((BS, BS), BF16)
         tab_finish()
         w_second()
@@ -481,12 +551,11 @@
         T1r.wait_recv()
         T6.start()
         T4.start()
+        c_relay(0)
         for copy in c_sends[1]:
             copy.start()
-        C3r[0].wait_recv()
-        C5[0].start()
-        C4r[0].wait_recv()
-        C6[0].start()
+        w_relay()
+        w_fourth()
         T5r.wait_recv()
         T7.start()
         T6r.wait_recv()
@@ -499,53 +568,34 @@
             copy.wait_recv()
         grads(0)
         pick(0)
-        AX[0].start()
-        BY[0].start()
-        C3r[1].wait_recv()
-        C5[1].start()
-        C4r[1].wait_recv()
-        C6[1].start()
-        w_fourth()
+        reduce_start(0)
+        c_relay(1)
+        w_load(0)
+        assemble(0)
+        hooks = o_hooks(0)
+        hooks[2] += [AX[0].middle, BY[0].middle]
+        forward(0, hooks)
+        o_relay(0)
         c_own[1].wait()
         for copy in c_recvs(1):
             copy.wait_recv()
         grads(1)
         pick(1)
-        AX[1].start()
-        BY[1].start()
-        AX[0].middle()
-        by_middle(0)
-        w_load(0)
-        assemble(0)
-        forward(0)
-        o_own[0].start()
-        for copy in o_sends[0]:
-            copy.start()
-        AX[1].middle()
-        by_middle(1)
+        reduce_start(1)
         ax_end(0)
         w_load(1)
         assemble(1)
-        forward(1)
-        o_own[1].start()
-        for copy in o_sends[1]:
-            copy.start()
-        by_end(0)
+        hooks = o_hooks(1)
+        hooks[1] += [lambda: by_end(0)]
+        hooks[2] += [AX[1].middle, BY[1].middle, AY[0].middle]
+        forward(1, hooks)
+        bx_middle(0)
+        ax_end(1)
+        o_relay(1)
         by_end(1)
-        ax_end(1)
-        AY[0].middle(LO, HI)
-        AY[1].middle(LO, HI)
-        O3r[0].wait_recv()
-        O5[0].start()
-        O4r[0].wait_recv()
-        O6[0].start()
-        bx_middle(0)
+        AY[1].middle()
+        finals(0)
         bx_middle(1)
-        O3r[1].wait_recv()
-        O5[1].start()
-        O4r[1].wait_recv()
-        O6[1].start()
-        finals(0)
         finals(1)
 
         for j in (0, 1):
@@ -574,16 +624,18 @@
 
             @pl.when(d[j] == 0)
             def _(j=j):
-                for copy in [W0[j], W1[j]] + V[j] + BX[j].sends():
+                for copy in [W0[j], W1[j], U0[j], U1[j]] + V[j] + BX[j].sends():
                     copy.wait_send()
 
             @pl.when(d[j] == 1)
             def _(j=j):
                 W2[j].wait_send()
+                U2[j].wait_send()
 
             @pl.when(d[j] == 3)
             def _(j=j):
                 W3[j].wait_send()
+                U3[j].wait_send()
 
             @pl.when(d[j] != 0)
             def _(j=j):
@@ -593,10 +645,10 @@
     return kernel
 
 
-def tables(slot_ids):
+def tables(slot_ids, live):
     numbers = jnp.arange(ROWS * 8, dtype=jnp.int32)
     block = jnp.where(numbers % 8 < COLS, (numbers // 8) * COLS + numbers % 8, -1)
-    match = (slot_ids[:, None] == block[None, :]).astype(jnp.int32)
+    match = ((slot_ids[:, None] == block[None, :]) & live[:, None]).astype(jnp.int32)
     index = jnp.sum(match * (jnp.arange(NSLOT, dtype=jnp.int32)[:, None] - NSLOT), axis=0) + NSLOT
     pad = ((0, 0), (0, 32 - SLOTS))
     ids = slot_ids.reshape(OWN, SLOTS)
@@ -606,9 +658,8 @@
 
 def shards(tokens, cotangent, master, block_ids, live_count):
     owners, slots = block_ids.shape
-    live_mask = (jnp.arange(slots, dtype=jnp.int32)[None, :] < live_count).astype(jnp.float32)
-    quantized = fake_quant(master, live_mask).reshape(owners * slots, BS, BS)
-    table = tables(block_ids.reshape(owners * slots))
+    live = jnp.arange(slots, dtype=jnp.int32)[None, :] < live_count
+    table = tables(block_ids.reshape(owners * slots), live.reshape(owners * slots))
     vmem = pltpu.VMEM
     blk = (BS, BS)
     anyspec = pl.BlockSpec(memory_space=pl.ANY)
@@ -641,14 +692,14 @@
             vmem((2, SLOTS) + blk, F32),
             vmem((2, 8, 128), jnp.int32),
             pltpu.SMEM((2, 8, 128), jnp.int32),
-            pltpu.SemaphoreType.DMA((112,)),
-            pltpu.SemaphoreType.DMA((112,)),
+            pltpu.SemaphoreType.DMA((144,)),
+            pltpu.SemaphoreType.DMA((144,)),
             pltpu.SemaphoreType.DMA((16,)),
         ],
         compiler_params=pltpu.CompilerParams(
             collective_id=0, has_side_effects=True, vmem_limit_bytes=66 * 1024 * 1000
         ),
-    )(tokens, cotangent, quantized, table)
+    )(tokens, cotangent, master.reshape(owners * slots, BS, BS), table)
     owner = lax.axis_index("dp") * lax.axis_size("seq") + lax.axis_index("seq")
     count = lax.dynamic_slice(live_count, (owner, 0), (1, 1))
     mine = jnp.arange(slots, dtype=jnp.int32)[None, :, None, None] < count[:, :, None, None]

time: 223 us -> 191 us (0.86)
  Pallas kernels: 200 us -> 178 us
  other arithmetic: 16 us -> 4.79 us
    pallas_call x1, Pallas kernels: 200 us -> 178 us  [shards(): pl.pallas_call(make_kernel(Names(), Names(), Names()), out_shape=(jax.Sha...]
    convert_element_type x2 -> x0, other arithmetic: 8.09 us -> none  [the longest x1 7.35 us: fake_quant(): (levels * (block_peak / 7.0) * live_mask[..., None, None]).astype(jnp.bfl...]
    reduce_max x1 -> x0, other arithmetic: 3.89 us -> none  [fake_quant(): jnp.max(jnp.abs(master_wide), axis=(-2, -1), keepdims=True) + 1e-06]
where the time goes in v2:
time: 191 us; the launch traced here: 190 us
  Pallas kernels  178 us (93%)
  local copies, waits for them, and re-layouts  7.14 us (4%)
  other arithmetic  4.79 us (3%)
    pallas_call x1, Pallas kernels, shards(): pl.pallas_call(make_kernel(Names(), Names(), Names()), out_shape=(jax.Sha...  178 us
    unnamed x1, local copies, waits for them, and re-layouts  4.2 us

profile of v2, /device:TPU:9, one launch (start us, length us, event | category | flops | bytes accessed | tf_op | source)
XLA Modules:
  0.0 190.5 jit_solution(8631491930175868583)
XLA Ops:
  0.6 0.7 pad.4
  1.3 0.1 reshape.70
  1.4 0.8 eq.18
  2.2 0.7 iota_compare_fusion
  2.9 0.1 lt.61
  3.0 0.2 select_reduce_fusion
  3.2 0.1 pad.7.clone
  3.2 0.7 add_add_fusion.tab_hbm
  3.9 177.9 %shard_map.68 = (bf16[128,14336]{1,0:T(8,128)(2,1)}, f32[21,128,128]{2,1,0:T(8,128)}, bf16[2,168,128,128]{3,2,1,0:T(8,128)(2,1)}) custom-call(bf16[128,4096]{1,0:T(8,128)(2,1)} %tok_hbm.1, bf16[128,14336]{1,0:T(8,128)(2,1)} %cot_hbm.1, bf16[168,128,128]{2,1,0:T(8,128)(2,1)} %bitcast.7, s32[8,128]{1,0:T(8,128)} %add_add_fusion.tab_hbm), custom_call_target="tpu_custom_call" | custom-call | tf_op jit(solution)/shard_map/pallas_call | solution.py:666
  181.8 1.2 constant_dynamic-slice_fusion
  183.1 0.6 iota_compare_fusion.1
  183.7 2.6 %select_bitcast_fusion = f32[1,21,128,128]{3,2,1,0:T(8,128)} fusion(f32[21,128,128]{2,1,0:T(8,128)} %get-tuple-element.5, pred[21]{0:T(512)(128)(4,1)S(1)} %iota_compare_fusion.1), kind=kLoop, calls=%fused_computation | loop fusion | flops 344064 | bytes 2752533 | tf_op jit(solution)/shard_map/jit(_where)/select_n | solution.py:706
  186.3 4.2 %copy.8 = bf16[128,14336]{1,0:T(8,128)(2,1)} copy(bf16[128,14336]{1,0:T(8,128)(2,1)} %get-tuple-element.8) | data formatting | bytes 7340032
  (4 shorter events, 0.0 us)

commit v3 on v2

--- a/solution.py
+++ b/solution.py
@@ -73,6 +73,7 @@
             ri = names_r.get(rkey or key, rwidth)
             if roff is not None:
                 ri = ri + roff
+            assert max(si, names_r.n) < 184
             return pltpu.make_async_remote_copy(
                 src_ref=src, dst_ref=dst, send_sem=ssem.at[si], recv_sem=rsem.at[ri],
                 device_id=devs[to], device_id_type=MESH,
@@ -292,7 +293,7 @@
             cp.start()
             cp.wait()
 
-        def grads(j):
+        def grads(j, hooks):
             @pl.loop(0, 16)
             def _(r):
                 rows = pl.ds(pl.multiple_of(r * 256, 256), 256)
@@ -301,6 +302,11 @@
                 for h in (0, 1):
                     for c in range(COLS):
                         gw[(r * 2 + h) * COLS + c] = g[h * BS:(h + 1) * BS, c * BS:(c + 1) * BS]
+                for at, steps in hooks.items():
+                    @pl.when(r == at)
+                    def _(steps=steps):
+                        for step in steps:
+                            step()
 
         def pick(j):
             for o in range(OWN):
@@ -385,9 +391,10 @@
                 self.c3l = remote(f"{name}3l", gs.at[j, base + xm, lo], second.at[1, lo], "x-")
                 self.c3h = remote(f"{name}3h", gs.at[j, base + xm, hi], second.at[1, hi], "x-")
 
-            def start(self):
-                for copy in (self.c0, self.c1, self.c2h, self.c3l):
-                    copy.start()
+            def start(self, which=(0, 1, 2)):
+                for i in which:
+                    for copy in ((self.c0, self.c1), (self.c2h,), (self.c3l,))[i]:
+                        copy.start()
 
             def middle(self):
                 self.c0.wait_recv()
@@ -466,13 +473,13 @@
         def add_ay(dst, src, half):
             add1(dst, src, (LO, HI)[half])
 
-        def add_by(dst, src, half):
-            for o in (0, 1):
-                add1(dst.at[o], src.at[o], SLOTS)
-
         AY = [YStage(f"Y{j}", j, gs.at[j, x], lo, hi, ry1, ry1.at[pl.ds(0, HI)], ry2, add_ay) for j in (0, 1)]
-        gs84 = [gs.at[j, pl.ds(4, 4)] for j in (0, 1)]
-        BY = [YStage(f"Z{j}", j, gs84[j], pl.ds(0, 2), pl.ds(2, 2), rz1, rz1, rz2, add_by) for j in (0, 1)]
+        order = (xo, xp, xm, x)
+        BY = [
+            [YStage(f"Z{j}{i}", j, gs.at[j, 4 + q], lo, hi, rz1.at[i], rz1.at[i, pl.ds(0, HI)], rz2.at[i], add_ay)
+             for i, q in enumerate(order)]
+            for j in (0, 1)
+        ]
         BX = [XStage(f"B{j}", j, 4, rb1, rb2) for j in (0, 1)]
 
         def ax_end(j):
@@ -480,13 +487,15 @@
             add2(gs.at[j, x], ra2.at[j, 0], ra2.at[j, 1], SLOTS)
             AY[j].start()
 
-        def by_end(j):
-            @pl.when(d[j] == 0)
-            def _():
-                BY[j].arrive()
-                for o in range(4):
-                    add2(gs84[j].at[o], rz2.at[0, o], rz2.at[1, o], SLOTS)
-                BX[j].start()
+        def by_end(j, i):
+            def go():
+                @pl.when(d[j] == 0)
+                def _():
+                    BY[j][i].arrive()
+                    add2(gs.at[j, 4 + order[i]], rz2.at[i, 0], rz2.at[i, 1], SLOTS)
+                    if i < 3:
+                        BX[j].start((i,))
+            return go
 
         def bx_middle(j):
             @pl.when(d[j] == 0)
@@ -532,7 +541,8 @@
 
         def reduce_start(j):
             AX[j].start()
-            BY[j].start()
+            for i in range(4):
+                BY[j][i].start()
 
         t_own.start()
         for copy in (T0, T1, T2):
@@ -566,36 +576,44 @@
         c_own[0].wait()
         for copy in c_recvs(0):
             copy.wait_recv()
-        grads(0)
+        grads(0, {})
         pick(0)
         reduce_start(0)
         c_relay(1)
+        c_own[1].wait()
+        for copy in c_recvs(1):
+            copy.wait_recv()
+        grads(1, {8: [BY[0][0].middle, BY[0][1].middle], 12: [AX[0].middle]})
+        pick(1)
+        reduce_start(1)
+        BY[0][2].middle()
+        BY[0][3].middle()
         w_load(0)
         assemble(0)
         hooks = o_hooks(0)
-        hooks[2] += [AX[0].middle, BY[0].middle]
+        hooks[1] += [lambda: ax_end(0)]
+        hooks[2] += [by_end(0, 0)]
+        hooks[3] += [AX[1].middle, AY[0].middle]
         forward(0, hooks)
-        o_relay(0)
-        c_own[1].wait()
-        for copy in c_recvs(1):
-            copy.wait_recv()
-        grads(1)
-        pick(1)
-        reduce_start(1)
-        ax_end(0)
         w_load(1)
         assemble(1)
+        o_relay(0)
         hooks = o_hooks(1)
-        hooks[1] += [lambda: by_end(0)]
-        hooks[2] += [AX[1].middle, BY[1].middle, AY[0].middle]
+        hooks[0] += [by_end(0, 1), by_end(0, 2), by_end(0, 3)]
+        hooks[1] += [BY[1][0].middle]
+        hooks[2] += [BY[1][1].middle, lambda: bx_middle(0)]
+        hooks[3] += [BY[1][2].middle]
         forward(1, hooks)
-        bx_middle(0)
         ax_end(1)
+        BY[1][3].middle()
+        by_end(1, 0)()
+        by_end(1, 1)()
         o_relay(1)
-        by_end(1)
+        by_end(1, 2)()
         AY[1].middle()
+        bx_middle(1)
+        by_end(1, 3)()
         finals(0)
-        bx_middle(1)
         finals(1)
 
         for j in (0, 1):
@@ -620,7 +638,8 @@
             for copy in c_sends[j] + [C5[j], C6[j]] + o_sends[j] + [O5[j], O6[j]] + AX[j].sends():
                 copy.wait_send()
             AY[j].wait_sends()
-            BY[j].wait_sends()
+            for i in range(4):
+                BY[j][i].wait_sends()
 
             @pl.when(d[j] == 0)
             def _(j=j):
@@ -685,25 +704,54 @@
             vmem((2, 2, SLOTS) + blk, BF16),
             vmem((LO,) + blk, BF16),
             vmem((2, SLOTS) + blk, BF16),
-            vmem((2, SLOTS) + blk, BF16),
-            vmem((2, 4, SLOTS) + blk, BF16),
+            vmem((4, LO) + blk, BF16),
+            vmem((4, 2, SLOTS) + blk, BF16),
             vmem((2, LO) + blk, BF16),
             vmem((2, SLOTS) + blk, BF16),
             vmem((2, SLOTS) + blk, F32),
             vmem((2, 8, 128), jnp.int32),
             pltpu.SMEM((2, 8, 128), jnp.int32),
-            pltpu.SemaphoreType.DMA((144,)),
-            pltpu.SemaphoreType.DMA((144,)),
+            pltpu.SemaphoreType.DMA((184,)),
+            pltpu.SemaphoreType.DMA((184,)),
             pltpu.SemaphoreType.DMA((16,)),
         ],
         compiler_params=pltpu.CompilerParams(
             collective_id=0, has_side_effects=True, vmem_limit_bytes=66 * 1024 * 1000
         ),
     )(tokens, cotangent, master.reshape(owners * slots, BS, BS), table)
-    owner = lax.axis_index("dp") * lax.axis_size("seq") + lax.axis_index("seq")
-    count = lax.dynamic_slice(live_count, (owner, 0), (1, 1))
-    mine = jnp.arange(slots, dtype=jnp.int32)[None, :, None, None] < count[:, :, None, None]
-    return (outputs, jnp.where(mine, w_grad[None], 0.0))
+    def finish_body(count_ref, o_ref, g_ref, o_out, g_out):
+        o_out[...] = o_ref[...]
+        own = count_ref[lax.axis_index("dp") * 4 + lax.axis_index("seq"), 0]
+        first = pl.program_id(0) * 3
+        for i in range(3):
+            keep = (first + i < own).astype(F32)
+            g_out[i] = g_ref[i] * keep
+
+    return finish(finish_body, live_count, outputs, w_grad)
+
+
+def finish(body, live_count, outputs, w_grad):
+    steps = 7
+    wide = outputs.shape[1] // steps
+    each = SLOTS // steps
+    outputs, w_grad = pl.pallas_call(
+        body,
+        grid=(steps,),
+        out_shape=(
+            jax.ShapeDtypeStruct(outputs.shape, outputs.dtype),
+            jax.ShapeDtypeStruct(w_grad.shape, w_grad.dtype),
+        ),
+        in_specs=[
+            pl.BlockSpec(memory_space=pltpu.SMEM),
+            pl.BlockSpec((outputs.shape[0], wide), lambda i: (0, i)),
+            pl.BlockSpec((each, BS, BS), lambda i: (i, 0, 0)),
+        ],
+        out_specs=(
+            pl.BlockSpec((outputs.shape[0], wide), lambda i: (0, i)),
+            pl.BlockSpec((each, BS, BS), lambda i: (i, 0, 0)),
+        ),
+    )(live_count, outputs, w_grad)
+    return outputs, w_grad[None]
 
 
 def solution(mesh):

time: 191 us -> 178 us (0.932)
  Pallas kernels: 178 us -> 172 us
  local copies, waits for them, and re-layouts: 7.14 us -> 3.03 us
  other arithmetic: 4.79 us -> 1.56 us
    pallas_call x1, Pallas kernels: 178 us -> 165 us  [shards(): pl.pallas_call(make_kernel(Names(), Names(), Names()), out_shape=(jax.Sha...]
    pallas_call x0 -> x1, Pallas kernels: none -> 7.17 us  [finish(): pl.pallas_call(body, grid=(steps,), out_shape=(jax.ShapeDtypeStruct(outpu...]
    unnamed x1, local copies, waits for them, and re-layouts: 4.2 us -> 1.32 us
    select_n x1 -> x0, other arithmetic: 2.58 us -> none  [shards(): return (outputs, jnp.where(mine, w_grad[None], 0.0))]
where the time goes in v3:
time: 178 us
  Pallas kernels  172 us (97%)
  local copies, waits for them, and re-layouts  3.03 us (2%)
    pallas_call x1, Pallas kernels, shards(): pl.pallas_call(make_kernel(Names(), Names(), Names()), out_shape=(jax.Sha...  165 us
    pallas_call x1, Pallas kernels, finish(): pl.pallas_call(body, grid=(steps,), out_shape=(jax.ShapeDtypeStruct(outpu...  7.17 us

profile of v3, /device:TPU:9, one launch (start us, length us, event | category | flops | bytes accessed | tf_op | source)
XLA Modules:
  0.0 177.5 jit_solution(4357648053737660714)
XLA Ops:
  0.6 0.7 iota_compare_fusion
  1.4 0.1 lt.43
  1.5 0.8 eq.18
  2.2 0.2 select_reduce_fusion
  2.4 0.7 pad.4
  3.1 0.1 reshape.59
  3.2 0.1 pad.7.clone
  3.2 0.7 add_add_fusion.tab_hbm
  3.9 165.1 %shard_map.68 = (bf16[128,14336]{1,0:T(8,128)(2,1)}, f32[21,128,128]{2,1,0:T(8,128)}, bf16[2,168,128,128]{3,2,1,0:T(8,128)(2,1)}) custom-call(bf16[128,4096]{1,0:T(8,128)(2,1)} %tok_hbm.1, bf16[128,14336]{1,0:T(8,128)(2,1)} %cot_hbm.1, bf16[168,128,128]{2,1,0:T(8,128)(2,1)} %bitcast.5, s32[8,128]{1,0:T(8,128)} %add_add_fusion.tab_hbm), custom_call_target="tpu_custom_call" | custom-call | tf_op jit(solution)/shard_map/pallas_call | solution.py:685
  169.0 1.3 copy.8.count_ref
  170.4 7.2 %shard_map.69 = (bf16[128,14336]{1,0:T(8,128)(2,1)}, f32[21,128,128]{2,1,0:T(8,128)}) custom-call(s32[8,1]{1,0:T(8,128)} %copy.8.count_ref, bf16[128,14336]{1,0:T(8,128)(2,1)} %get-tuple-element.6.o_ref, f32[21,128,128]{2,1,0:T(8,128)} %get-tuple-element.7.g_ref), custom_call_target="tpu_custom_call" | custom-call | tf_op jit(solution)/shard_map/pallas_call | solution.py:737
  (4 shorter events, 0.0 us)

commit v4 on v3

--- a/solution.py
+++ b/solution.py
@@ -289,9 +289,10 @@
                 U2[j].wait_recv()
                 U3[j].wait_recv()
 
-            cp = local("w", wc_hbm.at[j], wst.at[pl.ds(0, NSLOT)])
-            cp.start()
-            cp.wait()
+            local("w", wc_hbm.at[j], wst.at[pl.ds(0, NSLOT)]).start()
+
+        def w_ready(j):
+            local("w", wc_hbm.at[j], wst.at[pl.ds(0, NSLOT)]).wait()
 
         def grads(j, hooks):
             @pl.loop(0, 16)
@@ -320,8 +321,8 @@
                 for c in range(COLS):
                     gw[r * COLS + c] = wst[tabs[j, r // 16, (r % 16) * 8 + c]]
 
-        def forward(j, hooks):
-            @pl.loop(0, 4)
+        def forward(j, lo_m, hi_m, hooks):
+            @pl.loop(lo_m, hi_m)
             def _(m):
                 zz = (z + jnp.where(m == 0, 2, jnp.where(m == 1, 1, jnp.where(m == 2, 3, 0)))) % 4
                 rows = pl.ds(pl.multiple_of(zz * 256, 256), 256)
@@ -373,10 +374,11 @@
             def _(i):
                 dst[i] = (dst[i].astype(F32) + a[i].astype(F32) + b[i].astype(F32)).astype(BF16)
 
-        def sum3(out, dst, a, b, n):
-            @pl.loop(0, n)
+        def sum3(out, dst, a, b, count):
+            @pl.loop(0, SLOTS)
             def _(i):
-                out[i] = dst[i].astype(F32) + a[i].astype(F32) + b[i].astype(F32)
+                live = jnp.minimum(jnp.maximum(count - i, 0), 1).astype(F32)
+                out[i] = (dst[i].astype(F32) + a[i].astype(F32) + b[i].astype(F32)) * live
 
         lo, hi = pl.ds(0, LO), pl.ds(LO, HI)
 
@@ -509,9 +511,9 @@
             @pl.when(d[j] == 0)
             def _():
                 AY[j].arrive()
-                sum3(fin.at[0], gs.at[j, x], ry2.at[0], ry2.at[1], SLOTS)
+                sum3(fin.at[0], gs.at[j, x], ry2.at[0], ry2.at[1], tabs[j, 4, x])
                 BX[j].arrive()
-                sum3(fin.at[1], gs.at[j, 4 + x], rb2.at[0], rb2.at[1], SLOTS)
+                sum3(fin.at[1], gs.at[j, 4 + x], rb2.at[0], rb2.at[1], tabs[j, 4, 4 + x])
                 G.start()
                 g_own.start()
 
@@ -576,40 +578,41 @@
         c_own[0].wait()
         for copy in c_recvs(0):
             copy.wait_recv()
-        grads(0, {})
+        grads(0, {10: [lambda: c_relay(1)], 12: [lambda: w_load(0)]})
         pick(0)
         reduce_start(0)
-        c_relay(1)
+        w_ready(0)
+        assemble(0)
+        hooks = o_hooks(0)
+        hooks[1] += [BY[0][0].middle, BY[0][1].middle]
+        forward(0, 0, 2, hooks)
         c_own[1].wait()
         for copy in c_recvs(1):
             copy.wait_recv()
-        grads(1, {8: [BY[0][0].middle, BY[0][1].middle], 12: [AX[0].middle]})
+        grads(1, {4: [AX[0].middle, BY[0][2].middle], 8: [BY[0][3].middle]})
         pick(1)
         reduce_start(1)
-        BY[0][2].middle()
-        BY[0][3].middle()
-        w_load(0)
         assemble(0)
+        w_load(1)
         hooks = o_hooks(0)
-        hooks[1] += [lambda: ax_end(0)]
-        hooks[2] += [by_end(0, 0)]
-        hooks[3] += [AX[1].middle, AY[0].middle]
-        forward(0, hooks)
-        w_load(1)
+        hooks[2] += [lambda: ax_end(0)]
+        hooks[3] += [AX[1].middle, BY[1][0].middle]
+        forward(0, 2, 4, hooks)
+        w_ready(1)
         assemble(1)
+        AY[0].middle()
         o_relay(0)
+        for i in range(4):
+            by_end(0, i)()
         hooks = o_hooks(1)
-        hooks[0] += [by_end(0, 1), by_end(0, 2), by_end(0, 3)]
-        hooks[1] += [BY[1][0].middle]
-        hooks[2] += [BY[1][1].middle, lambda: bx_middle(0)]
-        hooks[3] += [BY[1][2].middle]
-        forward(1, hooks)
-        ax_end(1)
-        BY[1][3].middle()
-        by_end(1, 0)()
+        hooks[0] += [BY[1][1].middle]
+        hooks[1] += [BY[1][2].middle]
+        hooks[2] += [BY[1][3].middle, lambda: bx_middle(0)]
+        hooks[3] += [lambda: ax_end(1), by_end(1, 0)]
+        forward(1, 0, 4, hooks)
         by_end(1, 1)()
+        by_end(1, 2)()
         o_relay(1)
-        by_end(1, 2)()
         AY[1].middle()
         bx_middle(1)
         by_end(1, 3)()
@@ -664,7 +667,7 @@
     return kernel
 
 
-def tables(slot_ids, live):
+def tables(slot_ids, live, counts):
     numbers = jnp.arange(ROWS * 8, dtype=jnp.int32)
     block = jnp.where(numbers % 8 < COLS, (numbers // 8) * COLS + numbers % 8, -1)
     match = ((slot_ids[:, None] == block[None, :]) & live[:, None]).astype(jnp.int32)
@@ -672,13 +675,13 @@
     pad = ((0, 0), (0, 32 - SLOTS))
     ids = slot_ids.reshape(OWN, SLOTS)
     ids = jnp.pad(ids, pad).reshape(2, 128)
-    return jnp.concatenate([index.reshape(2, 128), ids, jnp.zeros((4, 128), jnp.int32)], axis=0)
+    return jnp.concatenate([index.reshape(2, 128), ids, jnp.pad(counts, ((0, 3), (0, 128 - OWN)))], axis=0)
 
 
 def shards(tokens, cotangent, master, block_ids, live_count):
     owners, slots = block_ids.shape
     live = jnp.arange(slots, dtype=jnp.int32)[None, :] < live_count
-    table = tables(block_ids.reshape(owners * slots), live.reshape(owners * slots))
+    table = tables(block_ids.reshape(owners * slots), live.reshape(owners * slots), live_count.reshape(1, owners))
     vmem = pltpu.VMEM
     blk = (BS, BS)
     anyspec = pl.BlockSpec(memory_space=pl.ANY)
@@ -719,38 +722,47 @@
             collective_id=0, has_side_effects=True, vmem_limit_bytes=66 * 1024 * 1000
         ),
     )(tokens, cotangent, master.reshape(owners * slots, BS, BS), table)
-    def finish_body(count_ref, o_ref, g_ref, o_out, g_out):
-        o_out[...] = o_ref[...]
-        own = count_ref[lax.axis_index("dp") * 4 + lax.axis_index("seq"), 0]
-        first = pl.program_id(0) * 3
-        for i in range(3):
-            keep = (first + i < own).astype(F32)
-            g_out[i] = g_ref[i] * keep
-
-    return finish(finish_body, live_count, outputs, w_grad)
-
-
-def finish(body, live_count, outputs, w_grad):
-    steps = 7
-    wide = outputs.shape[1] // steps
-    each = SLOTS // steps
+    return finish(outputs, w_grad)
+
+
+def finish(outputs, w_grad):
+    n_o, n_g = 8, 3
+    rows, each = outputs.shape[0] // n_o, SLOTS // n_g
+
+    def body(o_ref, g_ref, o_out, g_out, o_v, g_v, in_sem, out_sem):
+        loads, stores = [], []
+        for i in range(n_o):
+            part = pl.ds(i * rows, rows)
+            loads.append(pltpu.make_async_copy(o_ref.at[part], o_v.at[part], in_sem.at[i]))
+            stores.append(pltpu.make_async_copy(o_v.at[part], o_out.at[part], out_sem.at[i]))
+        for i in range(n_g):
+            part = pl.ds(i * each, each)
+            loads.append(pltpu.make_async_copy(g_ref.at[part], g_v.at[part], in_sem.at[n_o + i]))
+            stores.append(pltpu.make_async_copy(g_v.at[part], g_out.at[part], out_sem.at[n_o + i]))
+        for load in loads:
+            load.start()
+        for load, store in zip(loads, stores):
+            load.wait()
+            store.start()
+        for store in stores:
+            store.wait()
+
+    anyspec = pl.BlockSpec(memory_space=pl.ANY)
     outputs, w_grad = pl.pallas_call(
         body,
-        grid=(steps,),
         out_shape=(
             jax.ShapeDtypeStruct(outputs.shape, outputs.dtype),
             jax.ShapeDtypeStruct(w_grad.shape, w_grad.dtype),
         ),
-        in_specs=[
-            pl.BlockSpec(memory_space=pltpu.SMEM),
-            pl.BlockSpec((outputs.shape[0], wide), lambda i: (0, i)),
-            pl.BlockSpec((each, BS, BS), lambda i: (i, 0, 0)),
+        in_specs=[anyspec] * 2,
+        out_specs=(anyspec,) * 2,
+        scratch_shapes=[
+            pltpu.VMEM(outputs.shape, outputs.dtype),
+            pltpu.VMEM(w_grad.shape, w_grad.dtype),
+            pltpu.SemaphoreType.DMA((n_o + n_g,)),
+            pltpu.SemaphoreType.DMA((n_o + n_g,)),
         ],
-        out_specs=(
-            pl.BlockSpec((outputs.shape[0], wide), lambda i: (0, i)),
-            pl.BlockSpec((each, BS, BS), lambda i: (i, 0, 0)),
-        ),
-    )(live_count, outputs, w_grad)
+    )(outputs, w_grad)
     return outputs, w_grad[None]
 
 

time: 178 us -> 165 us (0.927)
  Pallas kernels: 172 us -> 161 us
    pallas_call x1, Pallas kernels: 165 us -> 156 us  [shards(): pl.pallas_call(make_kernel(Names(), Names(), Names()), out_shape=(jax.Sha...]
    pallas_call x1, Pallas kernels: 7.17 us -> 4.57 us  [finish(): pl.pallas_call(body, out_shape=(jax.ShapeDtypeStruct(outputs.shape, outpu...]
where the time goes in v4:
time: 165 us
  Pallas kernels  161 us (98%)
  other arithmetic  2.15 us (1%)
    pallas_call x1, Pallas kernels, shards(): pl.pallas_call(make_kernel(Names(), Names(), Names()), out_shape=(jax.Sha...  156 us
    pallas_call x1, Pallas kernels, finish(): pl.pallas_call(body, out_shape=(jax.ShapeDtypeStruct(outputs.shape, outpu...  4.57 us

profile of v4, /device:TPU:9, one launch (start us, length us, event | category | flops | bytes accessed | tf_op | source)
XLA Modules:
  0.0 165.1 jit_solution(1971636297038694862)
XLA Ops:
  0.6 0.7 iota_compare_fusion
  1.4 0.1 lt.43
  1.4 0.8 eq.18
  2.2 0.1 select_reduce_fusion
  2.4 0.7 pad.8
  3.1 0.1 reshape.62
  3.2 1.3 pad_add_fusion.tab_hbm
  4.4 156.1 %shard_map.68 = (bf16[128,14336]{1,0:T(8,128)(2,1)}, f32[21,128,128]{2,1,0:T(8,128)}, bf16[2,168,128,128]{3,2,1,0:T(8,128)(2,1)}) custom-call(bf16[128,4096]{1,0:T(8,128)(2,1)} %tok_hbm.1, bf16[128,14336]{1,0:T(8,128)(2,1)} %cot_hbm.1, bf16[168,128,128]{2,1,0:T(8,128)(2,1)} %bitcast.6, s32[8,128]{1,0:T(8,128)} %pad_add_fusion.tab_hbm), custom_call_target="tpu_custom_call" | custom-call | tf_op jit(solution)/shard_map/pallas_call | solution.py:688
  160.6 4.6 %shard_map.69 = (bf16[128,14336]{1,0:T(8,128)(2,1)}, f32[21,128,128]{2,1,0:T(8,128)}) custom-call(bf16[128,14336]{1,0:T(8,128)(2,1)} %get-tuple-element.6.o_ref, f32[21,128,128]{2,1,0:T(8,128)} %get-tuple-element.7.g_ref), custom_call_target="tpu_custom_call" | custom-call | tf_op jit(solution)/shard_map/pallas_call | solution.py:751
  (3 shorter events, 0.0 us)

commit v5 on v4

--- a/solution.py
+++ b/solution.py
@@ -8,6 +8,7 @@
 from jax.sharding import PartitionSpec as P
 
 BS = 128
+CUT = 512
 ROWS = 32
 COLS = 7
 OWN = 8
@@ -73,13 +74,14 @@
             ri = names_r.get(rkey or key, rwidth)
             if roff is not None:
                 ri = ri + roff
-            assert max(si, names_r.n) < 184
+            assert max(si, names_r.n) < 200
             return pltpu.make_async_remote_copy(
                 src_ref=src, dst_ref=dst, send_sem=ssem.at[si], recv_sem=rsem.at[ri],
                 device_id=devs[to], device_id_type=MESH,
             )
 
         def local(key, src, dst):
+            assert names_l.get(key) < 20
             return pltpu.make_async_copy(src, dst, lsem.at[names_l.get(key)])
 
         def slot(z_, k_):
@@ -121,34 +123,46 @@
         T7r = remote("T7", tok_v.at[part(zo, kk, 0)], tok_v.at[part(zo, kk, 0)], "p")
         T8r = remote("T8", tok_v.at[part(zo, kk, 64)], tok_v.at[part(zo, kk, 64)], "p")
 
-        def cot(group_y, group_z):
-            return cot_hbm.at[:, cols(group_y, group_z)]
-
-        c_own = [local(f"c{j}", cot(2 * k + j, z), cb.at[j, slot(z, k)]) for j in (0, 1)]
+        PARTS = ((0, 0, WID), (1, 0, CUT), (1, CUT, WID - CUT))
+
+        def cot(p, group_k, group_z):
+            j, c0, n = PARTS[p]
+            first = ((group_k * 2 + j) * 4 + group_z) * WID + c0
+            return cot_hbm.at[:, pl.ds(pl.multiple_of(first, 128), n)]
+
+        def cbuf(p, z_, k_):
+            j, c0, n = PARTS[p]
+            return cb.at[j, slot(z_, k_), pl.ds(c0, n)]
+
+        def crelay(p, way):
+            j, c0, n = PARTS[p]
+            return crel.at[way, j, :, pl.ds(c0, n)]
+
+        PS = (0, 1, 2)
+        c_own = [local(f"c{p}", cot(p, k, z), cbuf(p, z, k)) for p in PS]
         c_sends = []
-        for j in (0, 1):
-            row = []
-            row.append(remote(f"C3{j}", cot(j, zo), crel.at[0, j], "z+"))
-            row.append(remote(f"C4{j}", cot(2 + j, zo), crel.at[1, j], "z-"))
+        for p in PS:
+            row = [remote(f"C3{p}", cot(p, 0, zo), crelay(p, 0), "z+"), remote(f"C4{p}", cot(p, 1, zo), crelay(p, 1), "z-")]
             for k_ in (0, 1):
-                row.append(remote(f"C1{j}{k_}", cot(2 * k_ + j, zp), cb.at[j, slot(z, k)], f"z+{k_}",
-                                  rkey=f"C1r{j}", roff=k, rwidth=2))
-                row.append(remote(f"C2{j}{k_}", cot(2 * k_ + j, zm), cb.at[j, slot(z, k)], f"z-{k_}",
-                                  rkey=f"C2r{j}", roff=k, rwidth=2))
-            row.append(remote(f"C0{j}", cot(2 * kk + j, z), cb.at[j, slot(z, k)], "p"))
+                row.append(remote(f"C1{p}{k_}", cot(p, k_, zp), cbuf(p, z, k), f"z+{k_}", rkey=f"C1r{p}", roff=k, rwidth=2))
+                row.append(remote(f"C2{p}{k_}", cot(p, k_, zm), cbuf(p, z, k), f"z-{k_}", rkey=f"C2r{p}", roff=k, rwidth=2))
+            row.append(remote(f"C0{p}", cot(p, kk, z), cbuf(p, z, k), "p"))
             c_sends.append(row)
-        C3r = [remote(f"C3{j}", cot(j, zo), crel.at[0, j], "z+") for j in (0, 1)]
-        C4r = [remote(f"C4{j}", cot(2 + j, zo), crel.at[1, j], "z-") for j in (0, 1)]
-        C5 = [remote(f"C5{j}", crel.at[0, j], cb.at[j, slot(zm, k)], "z+0", rkey=f"C5r{j}", roff=k, rwidth=2) for j in (0, 1)]
-        C6 = [remote(f"C6{j}", crel.at[1, j], cb.at[j, slot(zp, k)], "z-1", rkey=f"C5r{j}", roff=k, rwidth=2) for j in (0, 1)]
-
-        def c_recvs(j):
-            out = [remote(f"C0{j}", cot(j, z), cb.at[j, slot(z, kk)], "p")]
+        C3r = [remote(f"C3{p}", cot(p, 0, zo), crelay(p, 0), "z+") for p in PS]
+        C4r = [remote(f"C4{p}", cot(p, 1, zo), crelay(p, 1), "z-") for p in PS]
+        C5 = [remote(f"C5{p}", crelay(p, 0), cbuf(p, zm, k), "z+0", rkey=f"C5r{p}", roff=k, rwidth=2) for p in PS]
+        C6 = [remote(f"C6{p}", crelay(p, 1), cbuf(p, zp, k), "z-1", rkey=f"C5r{p}", roff=k, rwidth=2) for p in PS]
+
+        def c_arrive(p):
+            src = cot(p, 0, z)
+            out = [remote(f"C0{p}", src, cbuf(p, z, kk), "p")]
             for i in (0, 1):
-                out.append(remote(f"C1{j}0", cot(j, z), cb.at[j, slot(zm, i)], "z+", rkey=f"C1r{j}", roff=i, rwidth=2))
-                out.append(remote(f"C2{j}0", cot(j, z), cb.at[j, slot(zp, i)], "z-", rkey=f"C2r{j}", roff=i, rwidth=2))
-                out.append(remote(f"C5{j}", cot(j, z), cb.at[j, slot(zo, i)], "z+", rkey=f"C5r{j}", roff=i, rwidth=2))
-            return out
+                out.append(remote(f"C1{p}0", src, cbuf(p, zm, i), "z+", rkey=f"C1r{p}", roff=i, rwidth=2))
+                out.append(remote(f"C2{p}0", src, cbuf(p, zp, i), "z-", rkey=f"C2r{p}", roff=i, rwidth=2))
+                out.append(remote(f"C5{p}", src, cbuf(p, zo, i), "z+", rkey=f"C5r{p}", roff=i, rwidth=2))
+            c_own[p].wait()
+            for copy in out:
+                copy.wait_recv()
 
         def wq(j, q):
             return wc_hbm.at[j, pl.ds(q * QTR, QTR)]
@@ -294,15 +308,19 @@
         def w_ready(j):
             local("w", wc_hbm.at[j], wst.at[pl.ds(0, NSLOT)]).wait()
 
-        def grads(j, hooks):
+        def grads(p, hooks):
+            j, c0, n = PARTS[p]
+
             @pl.loop(0, 16)
             def _(r):
                 rows = pl.ds(pl.multiple_of(r * 256, 256), 256)
-                g = lax.dot_general(tok_v[:, rows], cb[j], (((0,), (0,)), ((), ())), preferred_element_type=F32)
+                g = lax.dot_general(
+                    tok_v[:, rows], cb[j, :, c0:c0 + n], (((0,), (0,)), ((), ())), preferred_element_type=F32
+                )
                 g = g.astype(BF16)
                 for h in (0, 1):
-                    for c in range(COLS):
-                        gw[(r * 2 + h) * COLS + c] = g[h * BS:(h + 1) * BS, c * BS:(c + 1) * BS]
+                    for c in range(n // BS):
+                        gw[(r * 2 + h) * COLS + c0 // BS + c] = g[h * BS:(h + 1) * BS, c * BS:(c + 1) * BS]
                 for at, steps in hooks.items():
                     @pl.when(r == at)
                     def _(steps=steps):
@@ -564,7 +582,7 @@
         T6.start()
         T4.start()
         c_relay(0)
-        for copy in c_sends[1]:
+        for copy in c_sends[1] + c_sends[2]:
             copy.start()
         w_relay()
         w_fourth()
@@ -575,29 +593,24 @@
         t_own.wait()
         for copy in (T2r, T3r, T4r, T7r, T8r):
             copy.wait_recv()
-        c_own[0].wait()
-        for copy in c_recvs(0):
-            copy.wait_recv()
-        grads(0, {10: [lambda: c_relay(1)], 12: [lambda: w_load(0)]})
+        c_arrive(0)
+        grads(0, {4: [lambda: c_relay(1)], 10: [lambda: c_relay(2)], 13: [lambda: w_load(0)]})
         pick(0)
         reduce_start(0)
-        w_ready(0)
-        assemble(0)
-        hooks = o_hooks(0)
-        hooks[1] += [BY[0][0].middle, BY[0][1].middle]
-        forward(0, 0, 2, hooks)
-        c_own[1].wait()
-        for copy in c_recvs(1):
-            copy.wait_recv()
-        grads(1, {4: [AX[0].middle, BY[0][2].middle], 8: [BY[0][3].middle]})
+        c_arrive(1)
+        grads(1, {4: [BY[0][0].middle, BY[0][1].middle], 12: [AX[0].middle, BY[0][2].middle]})
+        c_arrive(2)
+        grads(2, {0: [BY[0][3].middle]})
         pick(1)
         reduce_start(1)
+        w_ready(0)
         assemble(0)
         w_load(1)
         hooks = o_hooks(0)
-        hooks[2] += [lambda: ax_end(0)]
-        hooks[3] += [AX[1].middle, BY[1][0].middle]
-        forward(0, 2, 4, hooks)
+        hooks[1] += [lambda: ax_end(0)]
+        hooks[2] += [AX[1].middle]
+        hooks[3] += [BY[1][0].middle]
+        forward(0, 0, 4, hooks)
         w_ready(1)
         assemble(1)
         AY[0].middle()
@@ -635,10 +648,10 @@
         def _():
             G.wait_recv()
 
-        for copy in (T0, T1, T2, T3, T4, T5, T6, T7, T8):
+        for copy in [T0, T1, T2, T3, T4, T5, T6, T7, T8] + c_sends[0] + c_sends[1] + c_sends[2] + C5 + C6:
             copy.wait_send()
         for j in (0, 1):
-            for copy in c_sends[j] + [C5[j], C6[j]] + o_sends[j] + [O5[j], O6[j]] + AX[j].sends():
+            for copy in o_sends[j] + [O5[j], O6[j]] + AX[j].sends():
                 copy.wait_send()
             AY[j].wait_sends()
             for i in range(4):
@@ -714,9 +727,9 @@
             vmem((2, SLOTS) + blk, F32),
             vmem((2, 8, 128), jnp.int32),
             pltpu.SMEM((2, 8, 128), jnp.int32),
-            pltpu.SemaphoreType.DMA((184,)),
-            pltpu.SemaphoreType.DMA((184,)),
-            pltpu.SemaphoreType.DMA((16,)),
+            pltpu.SemaphoreType.DMA((200,)),
+            pltpu.SemaphoreType.DMA((200,)),
+            pltpu.SemaphoreType.DMA((20,)),
         ],
         compiler_params=pltpu.CompilerParams(
             collective_id=0, has_side_effects=True, vmem_limit_bytes=66 * 1024 * 1000

time: 165 us -> 166 us (level)
  no operation moved by 1% of the time
where the time goes in v5:
time: 166 us
  Pallas kernels  162 us (98%)
  other arithmetic  2.15 us (1%)
    pallas_call x1, Pallas kernels, shards(): pl.pallas_call(make_kernel(Names(), Names(), Names()), out_shape=(jax.Sha...  157 us
    pallas_call x1, Pallas kernels, finish(): pl.pallas_call(body, out_shape=(jax.ShapeDtypeStruct(outputs.shape, outpu...  4.57 us

profile of v5, /device:TPU:9, one launch (start us, length us, event | category | flops | bytes accessed | tf_op | source)
XLA Modules:
  0.0 166.3 jit_solution(16156051566917634386)
XLA Ops:
  0.6 0.7 iota_compare_fusion
  1.4 0.1 lt.43
  1.4 0.8 eq.18
  2.2 0.1 select_reduce_fusion
  2.4 0.7 pad.8
  3.1 0.1 reshape.62
  3.2 1.3 pad_add_fusion.tab_hbm
  4.4 157.3 %shard_map.68 = (bf16[128,14336]{1,0:T(8,128)(2,1)}, f32[21,128,128]{2,1,0:T(8,128)}, bf16[2,168,128,128]{3,2,1,0:T(8,128)(2,1)}) custom-call(bf16[128,4096]{1,0:T(8,128)(2,1)} %tok_hbm.1, bf16[128,14336]{1,0:T(8,128)(2,1)} %cot_hbm.1, bf16[168,128,128]{2,1,0:T(8,128)(2,1)} %bitcast.6, s32[8,128]{1,0:T(8,128)} %pad_add_fusion.tab_hbm), custom_call_target="tpu_custom_call" | custom-call | tf_op jit(solution)/shard_map/pallas_call | solution.py:701
  161.7 4.6 %shard_map.69 = (bf16[128,14336]{1,0:T(8,128)(2,1)}, f32[21,128,128]{2,1,0:T(8,128)}) custom-call(bf16[128,14336]{1,0:T(8,128)(2,1)} %get-tuple-element.6.o_ref, f32[21,128,128]{2,1,0:T(8,128)} %get-tuple-element.7.g_ref), custom_call_target="tpu_custom_call" | custom-call | tf_op jit(solution)/shard_map/pallas_call | solution.py:764
  (3 shorter events, 0.0 us)

commit v6 on v4

--- a/solution.py
+++ b/solution.py
@@ -43,7 +43,7 @@
         tok_hbm, cot_hbm, q_hbm, tab_hbm,
         out_hbm, wg_hbm, wc_hbm,
         tok_v, cb, crel, gw, wst, ob, orel, gs, ra1, ra2, ry1, ry2, rz1, rz2, rb1, rb2, fin,
-        tabv, tabs, ssem, rsem, lsem,
+        tabv, tabs, invv, invs, ssem, rsem, lsem,
     ):
         k = lax.axis_index("dp")
         x = lax.axis_index("seq")
@@ -202,6 +202,15 @@
             cp = local("tab", tabv, tabs)
             cp.start()
             cp.wait()
+            spot = lax.broadcasted_iota(jnp.int32, (8, 128), 0) * 128 + lax.broadcasted_iota(jnp.int32, (8, 128), 1)
+            spot = jnp.where((spot & 7) < COLS, (spot >> 3) * COLS + (spot & 7), -1)
+            for j in (0, 1):
+                def slot_step(s, inv, j=j):
+                    for o in range(OWN):
+                        named = jnp.where(s < tabs[j, o, SLOTS], tabs[j, o, s], -2)
+                        inv = jnp.where(spot == named, o * SLOTS + s, inv)
+                    return inv
+                invv[j] = lax.fori_loop(0, SLOTS, slot_step, jnp.full((8, 128), NSLOT, jnp.int32))
 
         def quantize(j, start, n):
             @pl.loop(0, n // 4)
@@ -309,17 +318,16 @@
                         for step in steps:
                             step()
 
-        def pick(j):
-            for o in range(OWN):
-                @pl.loop(0, SLOTS)
-                def _(s, o=o):
-                    gs[j, o, s] = gw[tabs[j, 2 + o // 4, (o % 4) * 32 + s]]
+        def pick(j, o):
+            @pl.loop(0, SLOTS)
+            def _(s):
+                gs[j, o, s] = gw[tabs[j, o, s]]
 
         def assemble(j):
             @pl.loop(0, ROWS)
             def _(r):
                 for c in range(COLS):
-                    gw[r * COLS + c] = wst[tabs[j, r // 16, (r % 16) * 8 + c]]
+                    gw[r * COLS + c] = wst[invs[j, r // 16, (r % 16) * 8 + c]]
 
         def forward(j, lo_m, hi_m, hooks):
             @pl.loop(lo_m, hi_m)
@@ -507,15 +515,28 @@
         g_own = local("g", fin.at[k], wg_hbm)
         G = remote("G", fin.at[kk], wg_hbm, "p")
 
-        def finals(j):
+        def fin_out(half):
+            @pl.when(k == half)
+            def _():
+                g_own.start()
+
+            @pl.when(k != half)
+            def _():
+                G.start()
+
+        def final_a(j):
             @pl.when(d[j] == 0)
             def _():
                 AY[j].arrive()
-                sum3(fin.at[0], gs.at[j, x], ry2.at[0], ry2.at[1], tabs[j, 4, x])
+                sum3(fin.at[0], gs.at[j, x], ry2.at[0], ry2.at[1], tabs[j, x, SLOTS])
+                fin_out(0)
+
+        def final_b(j):
+            @pl.when(d[j] == 0)
+            def _():
                 BX[j].arrive()
-                sum3(fin.at[1], gs.at[j, 4 + x], rb2.at[0], rb2.at[1], tabs[j, 4, 4 + x])
-                G.start()
-                g_own.start()
+                sum3(fin.at[1], gs.at[j, 4 + x], rb2.at[0], rb2.at[1], tabs[j, 4 + x, SLOTS])
+                fin_out(1)
 
         def o_start(j, *which):
             def go():
@@ -542,8 +563,11 @@
             C6[j].start()
 
         def reduce_start(j):
-            AX[j].start()
-            for i in range(4):
+            for i, q in enumerate(order):
+                pick(j, q)
+                if i < 3:
+                    AX[j].start((i,))
+                pick(j, 4 + q)
                 BY[j][i].start()
 
         t_own.start()
@@ -563,6 +587,8 @@
         T1r.wait_recv()
         T6.start()
         T4.start()
+        inv = local("inv", invv, invs)
+        inv.start()
         c_relay(0)
         for copy in c_sends[1]:
             copy.start()
@@ -573,13 +599,13 @@
         T6r.wait_recv()
         T8.start()
         t_own.wait()
+        inv.wait()
         for copy in (T2r, T3r, T4r, T7r, T8r):
             copy.wait_recv()
         c_own[0].wait()
         for copy in c_recvs(0):
             copy.wait_recv()
         grads(0, {10: [lambda: c_relay(1)], 12: [lambda: w_load(0)]})
-        pick(0)
         reduce_start(0)
         w_ready(0)
         assemble(0)
@@ -590,7 +616,6 @@
         for copy in c_recvs(1):
             copy.wait_recv()
         grads(1, {4: [AX[0].middle, BY[0][2].middle], 8: [BY[0][3].middle]})
-        pick(1)
         reduce_start(1)
         assemble(0)
         w_load(1)
@@ -607,17 +632,21 @@
         hooks = o_hooks(1)
         hooks[0] += [BY[1][1].middle]
         hooks[1] += [BY[1][2].middle]
-        hooks[2] += [BY[1][3].middle, lambda: bx_middle(0)]
-        hooks[3] += [lambda: ax_end(1), by_end(1, 0)]
+        hooks[2] += [BY[1][3].middle]
+        hooks[3] += [lambda: ax_end(1)]
         forward(1, 0, 4, hooks)
+        by_end(1, 0)()
         by_end(1, 1)()
+        AY[1].middle()
+        bx_middle(0)
         by_end(1, 2)()
         o_relay(1)
-        AY[1].middle()
+        final_a(0)
         bx_middle(1)
         by_end(1, 3)()
-        finals(0)
-        finals(1)
+        final_b(0)
+        final_a(1)
+        final_b(1)
 
         for j in (0, 1):
             for copy in o_recvs(j):
@@ -667,21 +696,9 @@
     return kernel
 
 
-def tables(slot_ids, live, counts):
-    numbers = jnp.arange(ROWS * 8, dtype=jnp.int32)
-    block = jnp.where(numbers % 8 < COLS, (numbers // 8) * COLS + numbers % 8, -1)
-    match = ((slot_ids[:, None] == block[None, :]) & live[:, None]).astype(jnp.int32)
-    index = jnp.sum(match * (jnp.arange(NSLOT, dtype=jnp.int32)[:, None] - NSLOT), axis=0) + NSLOT
-    pad = ((0, 0), (0, 32 - SLOTS))
-    ids = slot_ids.reshape(OWN, SLOTS)
-    ids = jnp.pad(ids, pad).reshape(2, 128)
-    return jnp.concatenate([index.reshape(2, 128), ids, jnp.pad(counts, ((0, 3), (0, 128 - OWN)))], axis=0)
-
-
 def shards(tokens, cotangent, master, block_ids, live_count):
     owners, slots = block_ids.shape
-    live = jnp.arange(slots, dtype=jnp.int32)[None, :] < live_count
-    table = tables(block_ids.reshape(owners * slots), live.reshape(owners * slots), live_count.reshape(1, owners))
+    table = jnp.pad(block_ids, ((0, 0), (0, 128 - slots))) + jnp.pad(live_count, ((0, 0), (slots, 127 - slots)))
     vmem = pltpu.VMEM
     blk = (BS, BS)
     anyspec = pl.BlockSpec(memory_space=pl.ANY)
@@ -714,9 +731,11 @@
             vmem((2, SLOTS) + blk, F32),
             vmem((2, 8, 128), jnp.int32),
             pltpu.SMEM((2, 8, 128), jnp.int32),
+            vmem((2, 8, 128), jnp.int32),
+            pltpu.SMEM((2, 8, 128), jnp.int32),
             pltpu.SemaphoreType.DMA((184,)),
             pltpu.SemaphoreType.DMA((184,)),
-            pltpu.SemaphoreType.DMA((16,)),
+            pltpu.SemaphoreType.DMA((20,)),
         ],
         compiler_params=pltpu.CompilerParams(
             collective_id=0, has_side_effects=True, vmem_limit_bytes=66 * 1024 * 1000

time: 165 us -> 164 us (level); the launches traced: 165 us -> 162 us
  no operation moved by 1% of the time
where the time goes in v6:
time: 164 us; the launch traced here: 162 us
  Pallas kernels  160 us (98%)
    pallas_call x1, Pallas kernels, shards(): pl.pallas_call(make_kernel(Names(), Names(), Names()), out_shape=(jax.Sha...  155 us
    pallas_call x1, Pallas kernels, finish(): pl.pallas_call(body, out_shape=(jax.ShapeDtypeStruct(outputs.shape, outpu...  4.57 us

profile of v6, /device:TPU:9, one launch (start us, length us, event | category | flops | bytes accessed | tf_op | source)
XLA Modules:
  0.0 162.3 jit_solution(11181331958577258837)
XLA Ops:
  0.6 0.7 copy.7
  1.4 1.4 pad_add_fusion.tab_hbm
  2.7 155.0 %shard_map.68 = (bf16[128,14336]{1,0:T(8,128)(2,1)}, f32[21,128,128]{2,1,0:T(8,128)}, bf16[2,168,128,128]{3,2,1,0:T(8,128)(2,1)}) custom-call(bf16[128,4096]{1,0:T(8,128)(2,1)} %tok_hbm.1, bf16[128,14336]{1,0:T(8,128)(2,1)} %cot_hbm.1, bf16[168,128,128]{2,1,0:T(8,128)(2,1)} %bitcast.2, s32[8,128]{1,0:T(8,128)} %pad_add_fusion.tab_hbm), custom_call_target="tpu_custom_call" | custom-call | tf_op jit(solution)/shard_map/pallas_call | solution.py:705
  157.7 4.6 %shard_map.69 = (bf16[128,14336]{1,0:T(8,128)(2,1)}, f32[21,128,128]{2,1,0:T(8,128)}) custom-call(bf16[128,14336]{1,0:T(8,128)(2,1)} %get-tuple-element.6.o_ref, f32[21,128,128]{2,1,0:T(8,128)} %get-tuple-element.7.g_ref), custom_call_target="tpu_custom_call" | custom-call | tf_op jit(solution)/shard_map/pallas_call | solution.py:770

commit v7 on v6

--- a/solution.py
+++ b/solution.py
@@ -142,13 +142,18 @@
         C5 = [remote(f"C5{j}", crel.at[0, j], cb.at[j, slot(zm, k)], "z+0", rkey=f"C5r{j}", roff=k, rwidth=2) for j in (0, 1)]
         C6 = [remote(f"C6{j}", crel.at[1, j], cb.at[j, slot(zp, k)], "z-1", rkey=f"C5r{j}", roff=k, rwidth=2) for j in (0, 1)]
 
-        def c_recvs(j):
+        def c_near(j):
             out = [remote(f"C0{j}", cot(j, z), cb.at[j, slot(z, kk)], "p")]
             for i in (0, 1):
                 out.append(remote(f"C1{j}0", cot(j, z), cb.at[j, slot(zm, i)], "z+", rkey=f"C1r{j}", roff=i, rwidth=2))
                 out.append(remote(f"C2{j}0", cot(j, z), cb.at[j, slot(zp, i)], "z-", rkey=f"C2r{j}", roff=i, rwidth=2))
-                out.append(remote(f"C5{j}", cot(j, z), cb.at[j, slot(zo, i)], "z+", rkey=f"C5r{j}", roff=i, rwidth=2))
-            return out
+            c_own[j].wait()
+            for copy in out:
+                copy.wait_recv()
+
+        def c_far(j):
+            for i in (0, 1):
+                remote(f"C5{j}", cot(j, z), cb.at[j, slot(zo, i)], "z+", rkey=f"C5r{j}", roff=i, rwidth=2).wait_recv()
 
         def wq(j, q):
             return wc_hbm.at[j, pl.ds(q * QTR, QTR)]
@@ -303,15 +308,24 @@
         def w_ready(j):
             local("w", wc_hbm.at[j], wst.at[pl.ds(0, NSLOT)]).wait()
 
-        def grads(j, hooks):
+        def grads(j, chips, more, hooks):
             @pl.loop(0, 16)
             def _(r):
                 rows = pl.ds(pl.multiple_of(r * 256, 256), 256)
-                g = lax.dot_general(tok_v[:, rows], cb[j], (((0,), (0,)), ((), ())), preferred_element_type=F32)
-                g = g.astype(BF16)
+                g = None
+                for zz in chips:
+                    ks = pl.ds(pl.multiple_of(zz * 256, 256), 256)
+                    term = lax.dot_general(
+                        tok_v[ks, rows], cb[j, ks, :], (((0,), (0,)), ((), ())), preferred_element_type=F32
+                    )
+                    g = term if g is None else g + term
                 for h in (0, 1):
                     for c in range(COLS):
-                        gw[(r * 2 + h) * COLS + c] = g[h * BS:(h + 1) * BS, c * BS:(c + 1) * BS]
+                        at = (r * 2 + h) * COLS + c
+                        block = g[h * BS:(h + 1) * BS, c * BS:(c + 1) * BS]
+                        if more:
+                            block = block + gw[at].astype(F32)
+                        gw[at] = block.astype(BF16)
                 for at, steps in hooks.items():
                     @pl.when(r == at)
                     def _(steps=steps):
@@ -593,46 +607,46 @@
         for copy in c_sends[1]:
             copy.start()
         w_relay()
-        w_fourth()
+        t_own.wait()
+        inv.wait()
+        for copy in (T2r, T3r, T4r):
+            copy.wait_recv()
+        c_near(0)
+        near, far = (z, zp, zm), (zo,)
+        grads(0, near, False, {8: [w_fourth]})
         T5r.wait_recv()
         T7.start()
         T6r.wait_recv()
         T8.start()
-        t_own.wait()
-        inv.wait()
-        for copy in (T2r, T3r, T4r, T7r, T8r):
-            copy.wait_recv()
-        c_own[0].wait()
-        for copy in c_recvs(0):
-            copy.wait_recv()
-        grads(0, {10: [lambda: c_relay(1)], 12: [lambda: w_load(0)]})
+        T7r.wait_recv()
+        T8r.wait_recv()
+        c_far(0)
+        grads(0, far, True, {12: [lambda: c_relay(1)]})
         reduce_start(0)
+        w_load(0)
+        c_near(1)
+        grads(1, near, False, {6: [BY[0][0].middle], 10: [BY[0][1].middle], 13: [AX[0].middle]})
+        BY[0][2].middle()
+        c_far(1)
+        grads(1, far, True, {8: [BY[0][3].middle]})
+        reduce_start(1)
         w_ready(0)
-        assemble(0)
-        hooks = o_hooks(0)
-        hooks[1] += [BY[0][0].middle, BY[0][1].middle]
-        forward(0, 0, 2, hooks)
-        c_own[1].wait()
-        for copy in c_recvs(1):
-            copy.wait_recv()
-        grads(1, {4: [AX[0].middle, BY[0][2].middle], 8: [BY[0][3].middle]})
-        reduce_start(1)
         assemble(0)
         w_load(1)
         hooks = o_hooks(0)
-        hooks[2] += [lambda: ax_end(0)]
-        hooks[3] += [AX[1].middle, BY[1][0].middle]
-        forward(0, 2, 4, hooks)
+        hooks[0] += [lambda: ax_end(0)]
+        hooks[3] += [AX[1].middle, AY[0].middle]
+        forward(0, 0, 4, hooks)
         w_ready(1)
         assemble(1)
-        AY[0].middle()
-        o_relay(0)
         for i in range(4):
             by_end(0, i)()
+        BY[1][0].middle()
+        o_relay(0)
         hooks = o_hooks(1)
-        hooks[0] += [BY[1][1].middle]
-        hooks[1] += [BY[1][2].middle]
-        hooks[2] += [BY[1][3].middle]
+        hooks[1] += [BY[1][1].middle]
+        hooks[2] += [BY[1][2].middle]
+        hooks[3] += [BY[1][3].middle]
         hooks[3] += [lambda: ax_end(1)]
         forward(1, 0, 4, hooks)
         by_end(1, 0)()

time: 164 us -> 158 us (0.963)
  Pallas kernels: 160 us -> 154 us
    pallas_call x1, Pallas kernels: 155 us -> 149 us  [shards(): pl.pallas_call(make_kernel(Names(), Names(), Names()), out_shape=(jax.Sha...]
where the time goes in v7:
time: 158 us; the launch traced here: 157 us
  Pallas kernels  154 us (97%)
    pallas_call x1, Pallas kernels, shards(): pl.pallas_call(make_kernel(Names(), Names(), Names()), out_shape=(jax.Sha...  149 us
    pallas_call x1, Pallas kernels, finish(): pl.pallas_call(body, out_shape=(jax.ShapeDtypeStruct(outputs.shape, outpu...  4.57 us

profile of v7, /device:TPU:9, one launch (start us, length us, event | category | flops | bytes accessed | tf_op | source)
XLA Modules:
  0.0 156.7 jit_solution(493974338619050056)
XLA Ops:
  0.6 0.7 copy.7
  1.4 1.4 pad_add_fusion.tab_hbm
  2.7 149.4 %shard_map.68 = (bf16[128,14336]{1,0:T(8,128)(2,1)}, f32[21,128,128]{2,1,0:T(8,128)}, bf16[2,168,128,128]{3,2,1,0:T(8,128)(2,1)}) custom-call(bf16[128,4096]{1,0:T(8,128)(2,1)} %tok_hbm.1, bf16[128,14336]{1,0:T(8,128)(2,1)} %cot_hbm.1, bf16[168,128,128]{2,1,0:T(8,128)(2,1)} %bitcast.2, s32[8,128]{1,0:T(8,128)} %pad_add_fusion.tab_hbm), custom_call_target="tpu_custom_call" | custom-call | tf_op jit(solution)/shard_map/pallas_call | solution.py:719
  152.1 4.6 %shard_map.69 = (bf16[128,14336]{1,0:T(8,128)(2,1)}, f32[21,128,128]{2,1,0:T(8,128)}) custom-call(bf16[128,14336]{1,0:T(8,128)(2,1)} %get-tuple-element.6.o_ref, f32[21,128,128]{2,1,0:T(8,128)} %get-tuple-element.7.g_ref), custom_call_target="tpu_custom_call" | custom-call | tf_op jit(solution)/shard_map/pallas_call | solution.py:784

commit v8 on v7

--- a/solution.py
+++ b/solution.py
@@ -212,7 +212,7 @@
             for j in (0, 1):
                 def slot_step(s, inv, j=j):
                     for o in range(OWN):
-                        named = jnp.where(s < tabs[j, o, SLOTS], tabs[j, o, s], -2)
+                        named = jnp.where(s < tabs[j, 0, 32 + o], tabs[j, o, s], -2)
                         inv = jnp.where(spot == named, o * SLOTS + s, inv)
                     return inv
                 invv[j] = lax.fori_loop(0, SLOTS, slot_step, jnp.full((8, 128), NSLOT, jnp.int32))
@@ -542,14 +542,14 @@
             @pl.when(d[j] == 0)
             def _():
                 AY[j].arrive()
-                sum3(fin.at[0], gs.at[j, x], ry2.at[0], ry2.at[1], tabs[j, x, SLOTS])
+                sum3(fin.at[0], gs.at[j, x], ry2.at[0], ry2.at[1], tabs[j, 0, 32 + x])
                 fin_out(0)
 
         def final_b(j):
             @pl.when(d[j] == 0)
             def _():
                 BX[j].arrive()
-                sum3(fin.at[1], gs.at[j, 4 + x], rb2.at[0], rb2.at[1], tabs[j, 4 + x, SLOTS])
+                sum3(fin.at[1], gs.at[j, 4 + x], rb2.at[0], rb2.at[1], tabs[j, 0, 36 + x])
                 fin_out(1)
 
         def o_start(j, *which):
@@ -712,7 +712,7 @@
 
 def shards(tokens, cotangent, master, block_ids, live_count):
     owners, slots = block_ids.shape
-    table = jnp.pad(block_ids, ((0, 0), (0, 128 - slots))) + jnp.pad(live_count, ((0, 0), (slots, 127 - slots)))
+    table = jnp.pad(block_ids, ((0, 0), (0, 128 - slots))) + jnp.pad(live_count.reshape(1, owners), ((0, 7), (32, 96 - owners)))
     vmem = pltpu.VMEM
     blk = (BS, BS)
     anyspec = pl.BlockSpec(memory_space=pl.ANY)

time: 158 us -> 157 us (level)
  no operation moved by 1% of the time
where the time goes in v8:
time: 157 us; the launch traced here: 156 us
  Pallas kernels  154 us (98%)
    pallas_call x1, Pallas kernels, shards(): pl.pallas_call(make_kernel(Names(), Names(), Names()), out_shape=(jax.Sha...  149 us
    pallas_call x1, Pallas kernels, finish(): pl.pallas_call(body, out_shape=(jax.ShapeDtypeStruct(outputs.shape, outpu...  4.57 us

profile of v8, /device:TPU:9, one launch (start us, length us, event | category | flops | bytes accessed | tf_op | source)
XLA Modules:
  0.0 156.0 jit_solution(4583923428568120260)
XLA Ops:
  0.6 1.4 pad_add_fusion.tab_hbm
  2.0 149.4 %shard_map.68 = (bf16[128,14336]{1,0:T(8,128)(2,1)}, f32[21,128,128]{2,1,0:T(8,128)}, bf16[2,168,128,128]{3,2,1,0:T(8,128)(2,1)}) custom-call(bf16[128,4096]{1,0:T(8,128)(2,1)} %tok_hbm.1, bf16[128,14336]{1,0:T(8,128)(2,1)} %cot_hbm.1, bf16[168,128,128]{2,1,0:T(8,128)(2,1)} %bitcast.3, s32[8,128]{1,0:T(8,128)} %pad_add_fusion.tab_hbm), custom_call_target="tpu_custom_call" | custom-call | tf_op jit(solution)/shard_map/pallas_call | solution.py:719
  151.4 4.6 %shard_map.69 = (bf16[128,14336]{1,0:T(8,128)(2,1)}, f32[21,128,128]{2,1,0:T(8,128)}) custom-call(bf16[128,14336]{1,0:T(8,128)(2,1)} %get-tuple-element.6.o_ref, f32[21,128,128]{2,1,0:T(8,128)} %get-tuple-element.7.g_ref), custom_call_target="tpu_custom_call" | custom-call | tf_op jit(solution)/shard_map/pallas_call | solution.py:784
